TPU v7x, 32 devices: a whole 2x2x4 slice. The times are simulated.
32 devices in a mesh: dp: 16 (over z, y, core), fsdp: 2 (over x).
Axes of the slice: x: 2, y: 2, z: 4, core: 2. Of those that a mesh axis runs over, the one named last changes fastest.
Arguments:
- hidden_in: bfloat16 [4096, 1024], P(('dp', 'fsdp')), may hold values from -6 to 6
- doc_id: int32 [4096], P(('dp', 'fsdp')), may hold values from 0 to 128, as said below
- expert_ids: int32 [4096, 8], P(('dp', 'fsdp')), may hold values from 0 to 15, all different within a row
- out_grad: bfloat16 [4096, 1024], P(('dp', 'fsdp')), may hold values from -6 to 6
- attn_gain: bfloat16 [1024], P(('dp', 'fsdp')), may hold values from 0.5 to 1.5
- query_weight: bfloat16 [1024, 1024], P(('dp', 'fsdp')), may hold values from -0.1875 to 0.1875
- key_weight: bfloat16 [1024, 512], P(('dp', 'fsdp')), may hold values from -0.1875 to 0.1875
- value_weight: bfloat16 [1024, 512], P(('dp', 'fsdp')), may hold values from -0.1875 to 0.1875
- output_weight: bfloat16 [1024, 1024], P(('dp', 'fsdp')), may hold values from -0.75 to 0.75
- ffn_gain: bfloat16 [1024], P(('dp', 'fsdp')), may hold values from 0.5 to 1.5
- router_weight: bfloat16 [1024, 16], P(('dp', 'fsdp')), may hold values from -0.375 to 0.375
- expert_gate: bfloat16 [16, 1024, 512], P('dp', 'fsdp'), may hold values from -0.1875 to 0.1875
- expert_up: bfloat16 [16, 1024, 512], P('dp', 'fsdp'), may hold values from -0.1875 to 0.1875
- expert_down: bfloat16 [16, 512, 1024], P('dp', 'fsdp'), may hold values from -1 to 1
Outputs:
- layer_out: bfloat16 [4096, 1024], P(('dp', 'fsdp'))
- grad_in: bfloat16 [4096, 1024], P(('dp', 'fsdp'))
- grad_attn_gain: float32 [1024], P(('dp', 'fsdp'))
- grad_query: float32 [1024, 1024], P(('dp', 'fsdp'))
- grad_key: float32 [1024, 512], P(('dp', 'fsdp'))
- grad_value: float32 [1024, 512], P(('dp', 'fsdp'))
- grad_output: float32 [1024, 1024], P(('dp', 'fsdp'))
- grad_ffn_gain: float32 [1024], P(('dp', 'fsdp'))
- grad_router: float32 [1024, 16], P(('dp', 'fsdp'))
- grad_expert_gate: float32 [16, 1024, 512], P('dp', 'fsdp')
- grad_expert_up: float32 [16, 1024, 512], P('dp', 'fsdp')
- grad_expert_down: float32 [16, 512, 1024], P('dp', 'fsdp')
Inputs may be any that keep to these rules, and one draw needn't show every extreme that they name: Within each block of 128 rows doc_id starts at 0 and never falls; live rows come first and carry ids below 128; the rows after them carry 128 (padding). Every block has 64 or more live rows and some block has no padding. `expert_ids`: each row names 8 different experts.
All inputs are finite; a program needn't handle non-finite values.
Results may differ from a plain program's by a relative error of at most 0.015.
The roundings to bfloat16 on the way count: a program that leaves them out, or rounds other values in their place, can miss the bound.
Values may be sent and summed in bfloat16 or wider, within the bound.
A program may use at most 128 MiB of HBM per device.

v0:
```python
import functools

import jax
import jax.numpy as jnp
from jax import lax
from jax.experimental import pallas as pl
from jax.experimental.pallas import tpu as pltpu
from jax.sharding import PartitionSpec as P

HEADS = 16
KV_HEADS = 8
HEAD_DIM = 64
TOP = 8
CAP = 24


norm_eps = 1e-05


def positions_mask(doc_block):
    row_count = doc_block.shape[0]
    row_index = jnp.arange(row_count)
    same_doc = doc_block[:, None] == doc_block[None, :]
    earlier = row_index[None, :] < row_index[:, None]
    position = jnp.sum((same_doc & earlier).astype(jnp.float32), axis=1)
    allowed = same_doc & (row_index[None, :] <= row_index[:, None])
    live_rows = (doc_block < row_count).astype(jnp.float32)
    return (position, allowed, live_rows)


def rope_tables(position):
    half_dim = HEAD_DIM // 2
    freqs = jnp.exp(-jnp.log(10000.0) * (2.0 * jnp.arange(half_dim, dtype=jnp.float32) / HEAD_DIM))
    angle = position[:, None] * freqs[None, :]
    return (jnp.cos(angle), jnp.sin(angle))


def rotate(values, cosine, sinusoid):
    half_dim = values.shape[-1] // 2
    first_half, second_half = (values[..., :half_dim], values[..., half_dim:])
    return jnp.concatenate(
        [
            first_half * cosine - second_half * sinusoid,
            second_half * cosine + first_half * sinusoid,
        ],
        axis=-1,
    )


def unrotate(values, cosine, sinusoid):
    half_dim = values.shape[-1] // 2
    first_half, second_half = (values[..., :half_dim], values[..., half_dim:])
    return jnp.concatenate(
        [
            first_half * cosine + second_half * sinusoid,
            second_half * cosine - first_half * sinusoid,
        ],
        axis=-1,
    )


def norm_forward(values, gain):
    scale_row = lax.rsqrt(jnp.mean(values * values, axis=-1, keepdims=True) + norm_eps)
    normed = values * scale_row
    return (normed, scale_row, (normed * gain).astype(jnp.bfloat16))


def norm_backward(upstream, normed, scale_row, gain):
    scaled = upstream * gain
    inner = jnp.mean(scaled * normed, axis=-1, keepdims=True)
    return (scale_row * (scaled - normed * inner), jnp.sum(upstream * normed, axis=0))


def probabilities(query_b, key_b, allowed, log_total):
    scores = jnp.einsum(
        "ikgd,jkd->kgij", query_b, key_b, preferred_element_type=jnp.float32
    ) * HEAD_DIM ** (-0.5)
    raised = jnp.where(allowed[None, None], jnp.exp(scores), 0.0)
    if log_total is None:
        log_total = jnp.log(jnp.sum(raised, axis=-1, keepdims=True))
    return (jnp.where(allowed[None, None], jnp.exp(scores - log_total), 0.0), log_total)


def routing(expert_block, live_rows, logits):
    experts = logits.shape[1]
    row_count = expert_block.shape[0]
    chosen = jnp.sum(
        (expert_block[:, :, None] == jnp.arange(experts)[None, None, :]).astype(jnp.float32), axis=1
    )
    raised = jnp.where(chosen > 0, jnp.exp(logits), 0.0)
    gates = raised / jnp.sum(raised, axis=1, keepdims=True)
    member = chosen * live_rows[:, None]
    lower = (jnp.arange(row_count)[None, :] < jnp.arange(row_count)[:, None]).astype(jnp.float32)
    rank = jnp.dot(lower, member, precision=lax.Precision.HIGHEST)
    kept = member * (rank < CAP).astype(jnp.float32)
    slot_match = (rank.T[:, None, :] == jnp.arange(CAP, dtype=jnp.float32)[None, :, None]).astype(
        jnp.float32
    )
    dispatch = kept.T[:, None, :] * slot_match
    return (gates, dispatch, kept, rank)


def expert_forward(rows_in, w_gate, w_up, w_down):
    gate_pre = jnp.dot(rows_in, w_gate, preferred_element_type=jnp.float32)
    up_pre = jnp.dot(rows_in, w_up, preferred_element_type=jnp.float32)
    act_rows = (jax.nn.silu(gate_pre) * up_pre).astype(jnp.bfloat16)
    out_rows = jnp.dot(act_rows, w_down, preferred_element_type=jnp.float32).astype(jnp.bfloat16)
    return (gate_pre, up_pre, act_rows, out_rows)


def expert_backward(rows_in, gate_pre, up_pre, act_rows, grad_rows, w_gate, w_up, w_down):
    grad_act = jnp.dot(grad_rows, w_down.T, preferred_element_type=jnp.float32)
    sigmoid_gate = jax.nn.sigmoid(gate_pre)
    grad_up_pre = (grad_act * gate_pre * sigmoid_gate).astype(jnp.bfloat16)
    grad_gate_pre = (
        grad_act * up_pre * sigmoid_gate * (1.0 + gate_pre * (1.0 - sigmoid_gate))
    ).astype(jnp.bfloat16)
    grad_down_w = jnp.dot(act_rows.T, grad_rows, preferred_element_type=jnp.float32)
    grad_gate_w = jnp.dot(rows_in.T, grad_gate_pre, preferred_element_type=jnp.float32)
    grad_up_w = jnp.dot(rows_in.T, grad_up_pre, preferred_element_type=jnp.float32)
    grad_rows_in = jnp.dot(grad_gate_pre, w_gate.T, preferred_element_type=jnp.float32)
    grad_rows_in = (
        grad_rows_in + jnp.dot(grad_up_pre, w_up.T, preferred_element_type=jnp.float32)
    ).astype(jnp.bfloat16)
    return (grad_rows_in, grad_gate_w, grad_up_w, grad_down_w)


def axis_bits(size):
    return size.bit_length() - 1


def is_cube(sizes):
    return all(size & (size - 1) == 0 for size in sizes) and sizes[0] > 1


def span(bits):
    masks = [0]
    for bit in bits:
        masks = masks + [mask | (1 << bit) for mask in masks]
    return masks


def stream_orders(sizes):
    dp_bits, fsdp_bits = (axis_bits(sizes[0]), axis_bits(sizes[1]))
    low = [bit for bit in range(fsdp_bits)]
    high = [fsdp_bits + bit for bit in range(dp_bits - 1, 0, -1)]
    core = [fsdp_bits]
    return (high + low + core, high[:-1] + low + high[-1:] + core)


class Cube:
    def __init__(self, sizes):
        self.sizes = sizes
        self.dp = lax.axis_index("dp")
        self.fsdp = lax.axis_index("fsdp")
        self.me = self.dp * sizes[1] + self.fsdp
        self.fsdp_bits = axis_bits(sizes[1])
        self.flips = [
            (1 - 2 * ((self.me // (1 << bit)) % 2)) * (1 << bit)
            for bit in range(axis_bits(sizes[0]) + self.fsdp_bits)
        ]

    def block(self, mask):
        index = self.me
        for bit, flip in enumerate(self.flips):
            if mask >> bit & 1:
                index = index + flip
        return index

    def partner(self, bit):
        other = self.me + self.flips[bit]
        return {"dp": other // self.sizes[1], "fsdp": other % self.sizes[1]}

    def greet(self):
        barrier = pltpu.get_barrier_semaphore()
        for bit in range(len(self.flips)):
            pl.semaphore_signal(
                barrier, inc=1, device_id=self.partner(bit), device_id_type=pl.DeviceIdType.MESH
            )
        pl.semaphore_wait(barrier, len(self.flips))


def gather_kernel(sizes, a_ref, b_ref, a_out, b_out, local_sems, send_sems, recv_sems):
    cube = Cube(sizes)
    cube.greet()
    orders = stream_orders(sizes)
    streams = ((a_ref, a_out), (b_ref, b_out))
    copies = ({}, {})
    arrived = (set(), set())
    own = []
    for which, (source, target) in enumerate(streams):
        own.append(pltpu.make_async_copy(source, target.at[cube.me], local_sems.at[which]))
        own[-1].start()
    for stage in range(len(orders[0])):
        counts = len(span(orders[0][:stage]))
        for place in range(counts):
            for which, (source, target) in enumerate(streams):
                order = orders[which]
                mask = span(order[:stage])[place]
                if mask and mask not in arrived[which]:
                    copies[which][mask].wait_recv()
                    arrived[which].add(mask)
                label = mask | (1 << order[stage])
                copy = pltpu.make_async_remote_copy(
                    src_ref=target.at[cube.block(mask)] if mask else source,
                    dst_ref=target.at[cube.block(mask)],
                    send_sem=send_sems.at[which, label],
                    recv_sem=recv_sems.at[which, label],
                    device_id=cube.partner(order[stage]),
                    device_id_type=pl.DeviceIdType.MESH,
                )
                copy.start()
                copies[which][label] = copy
    for which in range(2):
        for label, copy in copies[which].items():
            if label not in arrived[which]:
                copy.wait_recv()
        for copy in copies[which].values():
            copy.wait_send()
        own[which].wait()


def gather_rows(sizes, packed_a, packed_b):
    blocks = sizes[0] * sizes[1]
    if not is_cube(sizes):
        return tuple(
            lax.all_gather(packed, ("dp", "fsdp"), axis=0) for packed in (packed_a, packed_b)
        )
    return pl.pallas_call(
        lambda *refs: gather_kernel(sizes, *refs),
        out_shape=tuple(
            jax.ShapeDtypeStruct((blocks,) + packed.shape, packed.dtype)
            for packed in (packed_a, packed_b)
        ),
        in_specs=[pl.BlockSpec(memory_space=pl.ANY)] * 2,
        out_specs=(pl.BlockSpec(memory_space=pl.ANY),) * 2,
        scratch_shapes=[
            pltpu.SemaphoreType.DMA((2,)),
            pltpu.SemaphoreType.DMA((2, blocks)),
            pltpu.SemaphoreType.DMA((2, blocks)),
        ],
        compiler_params=pltpu.CompilerParams(collective_id=0, has_side_effects=True),
        name="gather_rows",
    )(packed_a, packed_b)


def scatter_kernel(
    sizes, a_ref, b_ref, a_out, b_out, a_slots, b_slots, a_held, b_held, send_sems, recv_sems
):
    cube = Cube(sizes)
    cube.greet()
    orders = [order[::-1] for order in stream_orders(sizes)]
    streams = ((a_ref, a_out, a_slots, a_held), (b_ref, b_out, b_slots, b_held))
    copies = ({}, {})
    places = ({}, {})

    def total(which, mask, stage):
        source, _, slots, _ = streams[which]
        value = source[cube.block(mask)].astype(jnp.float32)
        for earlier in orders[which][:stage]:
            label = mask | (1 << earlier)
            copies[which][label].wait_recv()
            value = value + slots[label].astype(jnp.float32)
        return value

    for stage in range(len(orders[0])):
        for place in range(len(span(orders[0][stage + 1 :]))):
            for which, (source, _, slots, held) in enumerate(streams):
                order = orders[which]
                masks = span(order[stage + 1 :][::-1])
                masks.sort(
                    key=lambda mask: [
                        at for at, bit in enumerate(order) if mask >> bit & 1
                    ][:1]
                    or [len(order)]
                )
                mask = masks[place] | (1 << order[stage])
                if stage == 0:
                    leaving = source.at[cube.block(mask)]
                else:
                    slot = places[which].setdefault(mask, len(places[which]))
                    held[slot] = total(which, mask, stage).astype(jnp.bfloat16)
                    leaving = held.at[slot]
                copy = pltpu.make_async_remote_copy(
                    src_ref=leaving,
                    dst_ref=slots.at[mask],
                    send_sem=send_sems.at[which, mask],
                    recv_sem=recv_sems.at[which, mask],
                    device_id=cube.partner(order[stage]),
                    device_id_type=pl.DeviceIdType.MESH,
                )
                copy.start()
                copies[which][mask] = copy
    for which, (_, out, _, _) in enumerate(streams):
        out[...] = total(which, 0, len(orders[which]))
    for which in range(2):
        for copy in copies[which].values():
            copy.wait_send()


def scatter_rows(sizes, packed_a, packed_b):
    blocks = sizes[0] * sizes[1]
    if not is_cube(sizes):
        return tuple(
            lax.psum_scatter(packed.astype(jnp.float32), ("dp", "fsdp"), scatter_dimension=0)
            for packed in (packed_a, packed_b)
        )
    shapes = [packed.shape[1:] for packed in (packed_a, packed_b)]
    return pl.pallas_call(
        lambda *refs: scatter_kernel(sizes, *refs),
        out_shape=tuple(jax.ShapeDtypeStruct(shape, jnp.float32) for shape in shapes),
        in_specs=[pl.BlockSpec(memory_space=pltpu.VMEM)] * 2,
        out_specs=(pl.BlockSpec(memory_space=pltpu.VMEM),) * 2,
        scratch_shapes=[
            pltpu.VMEM((blocks,) + shapes[0], jnp.bfloat16),
            pltpu.VMEM((blocks,) + shapes[1], jnp.bfloat16),
            pltpu.VMEM((blocks // 2,) + shapes[0], jnp.bfloat16),
            pltpu.VMEM((blocks // 2,) + shapes[1], jnp.bfloat16),
            pltpu.SemaphoreType.DMA((2, blocks)),
            pltpu.SemaphoreType.DMA((2, blocks)),
        ],
        compiler_params=pltpu.CompilerParams(
            collective_id=1, has_side_effects=True, vmem_limit_bytes=48 * 1024 * 1024
        ),
        name="scatter_rows",
    )(packed_a, packed_b)


def shards(
    sizes,
    hidden_in,
    doc_id,
    expert_ids,
    out_grad,
    attn_gain,
    query_weight,
    key_weight,
    value_weight,
    output_weight,
    ffn_gain,
    router_weight,
    expert_gate,
    expert_up,
    expert_down,
):
    rows = hidden_in.shape[0]
    groups = HEADS // KV_HEADS
    scale = HEAD_DIM ** (-0.5)
    experts_all = router_weight.shape[1]
    query_width, key_width = (query_weight.shape[1], key_weight.shape[1])
    small_width = -(-(experts_all + 2) // 128) * 128
    small = jnp.concatenate([router_weight, attn_gain[:, None], ffn_gain[:, None]], axis=1)
    small = jnp.pad(small, ((0, 0), (0, small_width - small.shape[1])))
    full_a, full_b = gather_rows(
        sizes,
        jnp.concatenate([query_weight, key_weight, small], axis=1),
        jnp.concatenate([value_weight, output_weight], axis=1),
    )
    full_a = full_a.reshape(-1, full_a.shape[2])
    full_b = full_b.reshape(-1, full_b.shape[2])
    w_query = full_a[:, :query_width]
    w_key = full_a[:, query_width : query_width + key_width]
    full_small = full_a[:, query_width + key_width :]
    w_router = full_small[:, :experts_all]
    gain_one, gain_two = (full_small[:, experts_all], full_small[:, experts_all + 1])
    w_value = full_b[:, : value_weight.shape[1]]
    w_output = full_b[:, value_weight.shape[1] :]
    expert_full = (
        lax.all_gather(expert_gate, "fsdp", axis=1, tiled=True),
        lax.all_gather(expert_up, "fsdp", axis=1, tiled=True),
        lax.all_gather(expert_down, "fsdp", axis=1, tiled=True),
    )
    w_gate, w_up, w_down = (expert_full[0][0], expert_full[1][0], expert_full[2][0])
    position, allowed, live_rows = positions_mask(doc_id)
    cosine, sinusoid = rope_tables(position)
    cos_query, sin_query = (cosine[:, None, None, :], sinusoid[:, None, None, :])
    cos_key, sin_key = (cosine[:, None, :], sinusoid[:, None, :])
    resid_in = hidden_in.astype(jnp.float32)
    normed_one, scale_one, normed_in = norm_forward(resid_in, gain_one.astype(jnp.float32))
    query_raw = jnp.dot(normed_in, w_query, preferred_element_type=jnp.float32).reshape(
        rows, KV_HEADS, groups, HEAD_DIM
    )
    key_raw = jnp.dot(normed_in, w_key, preferred_element_type=jnp.float32).reshape(
        rows, KV_HEADS, HEAD_DIM
    )
    query_b = rotate(query_raw, cos_query, sin_query).astype(jnp.bfloat16)
    key_b = rotate(key_raw, cos_key, sin_key).astype(jnp.bfloat16)
    value_b = (
        jnp.dot(normed_in, w_value, preferred_element_type=jnp.float32)
        .reshape(rows, KV_HEADS, HEAD_DIM)
        .astype(jnp.bfloat16)
    )
    probs, log_total = probabilities(query_b, key_b, allowed, None)
    probs_b = probs.astype(jnp.bfloat16)
    mixed = jnp.einsum("kgij,jkd->ikgd", probs_b, value_b, preferred_element_type=jnp.float32)
    mixed_b = (
        (mixed * live_rows[:, None, None, None])
        .reshape(rows, HEADS * HEAD_DIM)
        .astype(jnp.bfloat16)
    )
    resid_mid = resid_in + jnp.dot(mixed_b, w_output, preferred_element_type=jnp.float32)
    normed_two, scale_two, routed_in = norm_forward(resid_mid, gain_two.astype(jnp.float32))
    logits = jnp.dot(routed_in, w_router, preferred_element_type=jnp.float32)
    gates, dispatch, kept, rank = routing(expert_ids, live_rows, logits)
    dispatch_b = dispatch.astype(jnp.bfloat16)
    send_rows = jnp.einsum(
        "ecr,rd->ecd", dispatch_b, routed_in, preferred_element_type=jnp.float32
    ).astype(jnp.bfloat16)
    recv_rows = lax.all_to_all(send_rows, "dp", split_axis=0, concat_axis=0, tiled=True)
    flat_in = recv_rows.reshape(-1, recv_rows.shape[2])
    gate_pre, up_pre, act_rows, out_rows = expert_forward(flat_in, w_gate, w_up, w_down)
    back_rows = lax.all_to_all(
        out_rows.reshape(recv_rows.shape), "dp", split_axis=0, concat_axis=0, tiled=True
    )
    experts = back_rows.shape[0]
    capacity = back_rows.shape[1]
    width = back_rows.shape[2]
    chosen_slot = (expert_ids[:, :, None] == jnp.arange(experts)[None, None, :]).astype(jnp.float32)
    gate_pick = jnp.sum(chosen_slot * (gates * kept)[:, None, :], axis=2)
    rank_pick = jnp.sum(chosen_slot * rank[:, None, :], axis=2)
    slot_index = expert_ids * capacity + jnp.minimum(rank_pick, capacity - 1.0).astype(jnp.int32)
    back_flat = back_rows.reshape(experts * capacity, width)
    picked_rows = jnp.take(back_flat, slot_index.reshape(-1), axis=0).reshape(rows, TOP, width)
    expert_sum = jnp.sum(gate_pick[:, :, None] * picked_rows.astype(jnp.float32), axis=1)
    layer_out = (resid_mid + expert_sum).astype(jnp.bfloat16)
    grad_out = out_grad.astype(jnp.float32)
    slot_gate = jnp.sum(dispatch * gates.T[:, None, :], axis=2)
    pulled_grad = jnp.einsum(
        "ecr,rd->ecd", dispatch_b, out_grad, preferred_element_type=jnp.float32
    )
    grad_send = (slot_gate[:, :, None] * pulled_grad).astype(jnp.bfloat16)
    slot_dot = jnp.sum(back_rows.astype(jnp.float32) * pulled_grad, axis=2)
    grad_gates = jnp.sum(dispatch * slot_dot[:, :, None], axis=1).T
    grad_logits = gates * (grad_gates - jnp.sum(gates * grad_gates, axis=1, keepdims=True))
    grad_logits_b = grad_logits.astype(jnp.bfloat16)
    grad_recv = lax.all_to_all(grad_send, "dp", split_axis=0, concat_axis=0, tiled=True)
    grad_rows_in, grad_gate_w, grad_up_w, grad_down_w = expert_backward(
        flat_in, gate_pre, up_pre, act_rows, grad_recv.reshape(flat_in.shape), w_gate, w_up, w_down
    )
    grad_back = lax.all_to_all(
        grad_rows_in.reshape(recv_rows.shape), "dp", split_axis=0, concat_axis=0, tiled=True
    )
    grad_routed = jnp.einsum(
        "ecr,ecd->rd", dispatch_b, grad_back, preferred_element_type=jnp.float32
    )
    grad_routed = grad_routed + jnp.dot(
        grad_logits_b, w_router.T, preferred_element_type=jnp.float32
    )
    grad_w_router = jnp.dot(routed_in.T, grad_logits_b, preferred_element_type=jnp.float32)
    grad_norm_two, grad_gain_two = norm_backward(
        grad_routed, normed_two, scale_two, gain_two.astype(jnp.float32)
    )
    grad_mid = grad_out + grad_norm_two
    grad_mid_b = grad_mid.astype(jnp.bfloat16)
    grad_w_output = jnp.dot(mixed_b.T, grad_mid_b, preferred_element_type=jnp.float32)
    grad_mixed = jnp.dot(grad_mid_b, w_output.T, preferred_element_type=jnp.float32).reshape(
        rows, KV_HEADS, groups, HEAD_DIM
    )
    grad_mixed = (grad_mixed * live_rows[:, None, None, None]).astype(jnp.bfloat16)
    probs_again, unused_total = probabilities(query_b, key_b, allowed, log_total)
    grad_probs = jnp.einsum(
        "ikgd,jkd->kgij", grad_mixed, value_b, preferred_element_type=jnp.float32
    )
    delta = jnp.sum(probs_again * grad_probs, axis=-1, keepdims=True)
    grad_scores = (probs_again * (grad_probs - delta) * scale).astype(jnp.bfloat16)
    grad_query_raw = jnp.einsum(
        "kgij,jkd->ikgd", grad_scores, key_b, preferred_element_type=jnp.float32
    )
    grad_key_raw = jnp.einsum(
        "kgij,ikgd->jkd", grad_scores, query_b, preferred_element_type=jnp.float32
    )
    grad_value_raw = jnp.einsum(
        "kgij,ikgd->jkd",
        probs_again.astype(jnp.bfloat16),
        grad_mixed,
        preferred_element_type=jnp.float32,
    )
    grad_query_b = (
        unrotate(grad_query_raw, cos_query, sin_query)
        .reshape(rows, HEADS * HEAD_DIM)
        .astype(jnp.bfloat16)
    )
    grad_key_b = (
        unrotate(grad_key_raw, cos_key, sin_key)
        .reshape(rows, KV_HEADS * HEAD_DIM)
        .astype(jnp.bfloat16)
    )
    grad_value_b = grad_value_raw.reshape(rows, KV_HEADS * HEAD_DIM).astype(jnp.bfloat16)
    grad_w_query = jnp.dot(normed_in.T, grad_query_b, preferred_element_type=jnp.float32)
    grad_w_key = jnp.dot(normed_in.T, grad_key_b, preferred_element_type=jnp.float32)
    grad_w_value = jnp.dot(normed_in.T, grad_value_b, preferred_element_type=jnp.float32)
    grad_normed = jnp.dot(grad_query_b, w_query.T, preferred_element_type=jnp.float32)
    grad_normed = grad_normed + jnp.dot(grad_key_b, w_key.T, preferred_element_type=jnp.float32)
    grad_normed = grad_normed + jnp.dot(grad_value_b, w_value.T, preferred_element_type=jnp.float32)
    grad_norm_one, grad_gain_one = norm_backward(
        grad_normed, normed_one, scale_one, gain_one.astype(jnp.float32)
    )
    grad_input = (grad_mid + grad_norm_one).astype(jnp.bfloat16)
    grad_small = jnp.concatenate(
        [grad_w_router, grad_gain_one[:, None], grad_gain_two[:, None]], axis=1
    )
    grad_small = jnp.pad(grad_small, ((0, 0), (0, small_width - grad_small.shape[1])))
    blocks = sizes[0] * sizes[1]
    own_a, own_b = scatter_rows(
        sizes,
        jnp.concatenate(
            [
                grad_w_query.astype(jnp.bfloat16),
                grad_w_key.astype(jnp.bfloat16),
                grad_small.astype(jnp.bfloat16),
            ],
            axis=1,
        ).reshape(blocks, -1, full_a.shape[1]),
        jnp.concatenate(
            [grad_w_value.astype(jnp.bfloat16), grad_w_output.astype(jnp.bfloat16)], axis=1
        ).reshape(blocks, -1, full_b.shape[1]),
    )
    own_small = own_a[:, query_width + key_width :]
    dense_grads = (
        own_small[:, experts_all],
        own_a[:, :query_width],
        own_a[:, query_width : query_width + key_width],
        own_b[:, : value_weight.shape[1]],
        own_b[:, value_weight.shape[1] :],
        own_small[:, experts_all + 1],
        own_small[:, :experts_all],
    )
    expert_grads = (
        lax.psum_scatter(
            grad_gate_w[None].astype(jnp.bfloat16), "fsdp", scatter_dimension=1, tiled=True
        ).astype(jnp.float32),
        lax.psum_scatter(
            grad_up_w[None].astype(jnp.bfloat16), "fsdp", scatter_dimension=1, tiled=True
        ).astype(jnp.float32),
        lax.psum_scatter(
            grad_down_w[None].astype(jnp.bfloat16), "fsdp", scatter_dimension=1, tiled=True
        ).astype(jnp.float32),
    )
    return (
        layer_out,
        grad_input,
        dense_grads[0],
        dense_grads[1],
        dense_grads[2],
        dense_grads[3],
        dense_grads[4],
        dense_grads[5],
        dense_grads[6],
        expert_grads[0],
        expert_grads[1],
        expert_grads[2],
    )


def solution(mesh):
    in_specs = (
        P(("dp", "fsdp"), None),
        P(("dp", "fsdp")),
        P(("dp", "fsdp"), None),
        P(("dp", "fsdp"), None),
        P(("dp", "fsdp")),
        P(("dp", "fsdp"), None),
        P(("dp", "fsdp"), None),
        P(("dp", "fsdp"), None),
        P(("dp", "fsdp"), None),
        P(("dp", "fsdp")),
        P(("dp", "fsdp"), None),
        P("dp", "fsdp", None),
        P("dp", "fsdp", None),
        P("dp", "fsdp", None),
    )
    out_specs = (
        P(("dp", "fsdp"), None),
        P(("dp", "fsdp"), None),
        P(("dp", "fsdp")),
        P(("dp", "fsdp"), None),
        P(("dp", "fsdp"), None),
        P(("dp", "fsdp"), None),
        P(("dp", "fsdp"), None),
        P(("dp", "fsdp")),
        P(("dp", "fsdp"), None),
        P("dp", "fsdp", None),
        P("dp", "fsdp", None),
        P("dp", "fsdp", None),
    )
    sizes = (mesh.shape["dp"], mesh.shape["fsdp"])
    body = functools.partial(shards, sizes)
    return jax.shard_map(body, mesh=mesh, in_specs=in_specs, out_specs=out_specs, check_vma=False)
```

profile of v0, /device:TPU:0, one launch (start us, length us, event | category | flops | bytes accessed | tf_op | source)
XLA Modules:
  0.0 304.5 jit_solution(4583631271340262861)
XLA Ops:
  12.4 1.5 pad_maximum_fusion.8.refs_1_
  14.0 1.5 pad_maximum_fusion.7.refs_0_
  15.5 58.0 %gather_rows.1 = (bf16[32,32,1664]{2,1,0:T(8,128)(2,1)}, bf16[32,32,1536]{2,1,0:T(8,128)(2,1)}) custom-call(bf16[32,1664]{1,0:T(8,128)(2,1)} %pad_maximum_fusion.7.refs_0_, bf16[32,1536]{1,0:T(8,128)(2,1)} %pad_maximum_fusion.8.refs_1_), custom_call_target="tpu_custom_call" | custom-call | tf_op jit(solution)/shard_map/gather_rows/pallas_call | solution.py:229
  73.5 1.2 slice_convert_fusion
  75.1 2.6 fusion.8
  77.7 1.8 fusion.45
  79.7 1.6 convolution_convert_fusion.9
  83.1 2.2 multiply_reduce_fusion.5
  85.9 1.2 convolution_convert_fusion.8
  87.1 5.2 %all-to-all-start = ((bf16[16,24,1024]{2,1,0:T(8,128)(2,1)}), bf16[16,24,1024]{2,1,0:T(8,128)(2,1)S(1)}, u32[]{:S(2)}, u32[]{:S(2)}) async-start(bf16[16,24,1024]{2,1,0:T(8,128)(2,1)} %convolution_convert_fusion.8), calls=%async_computation | async-start | bytes 1572864 | tf_op jit(solution)/shard_map/all_to_all | solution.py:409
  93.0 17.9 %all-to-all-done = bf16[16,24,1024]{2,1,0:T(8,128)(2,1)S(1)} async-done(((bf16[16,24,1024]{2,1,0:T(8,128)(2,1)}), bf16[16,24,1024]{2,1,0:T(8,128)(2,1)S(1)}, u32[]{:S(2)}, u32[]{:S(2)}) %all-to-all-start) | async-done | bytes 786464 | tf_op jit(solution)/shard_map/all_to_all | solution.py:409
  110.9 1.8 fusion.36
  113.7 2.7 multiply_convert_fusion.3
  116.3 2.9 convolution_convert_fusion.7
  119.2 5.4 %all-to-all-start.1 = ((bf16[16,24,1024]{2,1,0:T(8,128)(2,1)}), bf16[16,24,1024]{2,1,0:T(8,128)(2,1)S(1)}, u32[]{:S(2)}, u32[]{:S(2)}) async-start(bf16[16,24,1024]{2,1,0:T(8,128)(2,1)} %bitcast.23), calls=%async_computation.1 | async-start | bytes 1572864 | tf_op jit(solution)/shard_map/all_to_all | solution.py:412
  124.7 1.2 fusion.123
  125.9 17.4 %all-to-all-done.1 = bf16[16,24,1024]{2,1,0:T(8,128)(2,1)S(1)} async-done(((bf16[16,24,1024]{2,1,0:T(8,128)(2,1)}), bf16[16,24,1024]{2,1,0:T(8,128)(2,1)S(1)}, u32[]{:S(2)}, u32[]{:S(2)}) %all-to-all-start.1) | async-done | bytes 786464 | tf_op jit(solution)/shard_map/all_to_all | solution.py:412
  144.2 25.3 %all_to_all.20 = bf16[16,24,1024]{2,1,0:T(8,128)(2,1)S(1)} all-to-all(bf16[16,24,1024]{2,1,0:T(8,128)(2,1)S(1)} %multiply_convert_fusion), channel_id=1, replica_groups=mesh['dp'=16,'fsdp'=2] {'dp'}, dimensions={0} | all-to-all | bytes 1572864 | tf_op jit(solution)/shard_map/all_to_all | solution.py:436
  169.5 1.7 multiply_convert_fusion.1
  171.1 1.7 fusion.10
  172.9 2.9 fusion.19
  176.5 2.8 fusion.11
  179.3 1.7 fusion.34
  181.0 1.5 add_convert_fusion
  182.5 4.3 %all-to-all-start.3 = ((bf16[16,24,1024]{2,1,0:T(8,128)(2,1)}), bf16[16,24,1024]{2,1,0:T(8,128)(2,1)}, u32[]{:S(2)}, u32[]{:S(2)}) async-start(bf16[16,24,1024]{2,1,0:T(8,128)(2,1)} %bitcast.30), calls=%async_computation.3 | async-start | bytes 1572864 | tf_op jit(solution)/shard_map/all_to_all | solution.py:440
  189.4 4.5 %gather_fusion = bf16[1024,1024]{1,0:T(8,128)(2,1)S(1)} fusion(bf16[384,1024]{1,0:T(8,128)(2,1)S(1)} %bitcast.134, s32[1024]{0:T(1024)} %broadcast_clamp_fusion), kind=kCustom, calls=%fused_computation | custom fusion | bytes 4198400 | tf_op jit(solution)/shard_map/jit(_take)/gather | solution.py:423
  193.9 1.5 convolution_convert_fusion.10
  195.5 3.2 %multiply_reduce_fusion = f32[128,1024]{1,0:T(8,128)} fusion(bf16[1024,1024]{1,0:T(8,128)(2,1)S(1)} %gather_fusion, f32[128,8]{1,0:T(8,128)} %copy.77, pred[128,8]{1,0:T(8,128)(4,1)} %copy.78), kind=kLoop, calls=%fused_computation.3 | loop fusion | flops 4063232 | bytes 2626560 | tf_op jit(solution)/shard_map/reduce_sum | solution.py:424
  198.8 1.8 fusion.12
  200.6 4.9 %all-to-all-done.3 = bf16[16,24,1024]{2,1,0:T(8,128)(2,1)} async-done(((bf16[16,24,1024]{2,1,0:T(8,128)(2,1)}), bf16[16,24,1024]{2,1,0:T(8,128)(2,1)}, u32[]{:S(2)}, u32[]{:S(2)}) %all-to-all-start.3) | async-done | bytes 786464 | tf_op jit(solution)/shard_map/all_to_all | solution.py:440
  205.5 1.6 convolution_bitcast_fusion.2
  207.2 1.3 multiply_reduce_fusion.3
  210.7 2.0 convolution_bitcast_fusion.1
  212.7 2.0 convolution_bitcast_fusion.4
  214.7 2.1 fusion.26
  216.9 2.4 fusion.6
  220.0 1.7 convolution_add_fusion.1
  221.7 2.7 fusion.59
  225.7 3.6 %copy.84 = bf16[1024,1664]{1,0:T(8,128)(2,1)} copy(bf16[1024,1664]{0,1:T(8,128)(2,1)S(1)} %pad_maximum_fusion) | data formatting | bytes 6815744 | tf_op jit(solution)/shard_map/concatenate | solution.py:506
  229.4 1.5 convolution_convert_fusion.2
  230.9 1.9 convolution_convert_fusion.1
  232.8 2.0 pad_maximum_fusion.1
  234.8 3.4 %copy.85 = bf16[1024,1536]{1,0:T(8,128)(2,1)S(1)} copy(bf16[1024,1536]{0,1:T(8,128)(2,1)} %pad_maximum_fusion.1) | data formatting | bytes 6291456 | tf_op jit(solution)/shard_map/concatenate | solution.py:514
  238.2 46.8 %scatter_rows.1 = (f32[32,1664]{1,0:T(8,128)S(1)}, f32[32,1536]{1,0:T(8,128)S(1)}) custom-call(bf16[32,32,1664]{2,1,0:T(8,128)(2,1)} %bitcast.135, bf16[32,32,1536]{2,1,0:T(8,128)(2,1)S(1)} %bitcast.133), custom_call_target="tpu_custom_call" | custom-call | tf_op jit(solution)/shard_map/scatter_rows/pallas_call | solution.py:309
  289.0 2.2 fusion.58
  291.2 2.1 convert_element_type.225
  293.4 2.1 convert_element_type.228
  295.5 2.1 convert_element_type.231
  (182 shorter events, 21.7 us)
Async XLA Ops:
  7.2 67.8 %copy-start = (bf16[128,1024]{1,0:T(8,128)(2,1)S(1)}, bf16[128,1024]{1,0:T(8,128)(2,1)}, u32[]{:S(2)}) copy-start(bf16[128,1024]{1,0:T(8,128)(2,1)} %param.14) | copy-start | bytes 786436
  7.2 85.8 %all-gather.4.cloned.1.call-start = ((), (), s32[]{:S(2)}) async-start(), calls=%async_computation.7 | async-start | bytes 1572864 | tf_op jit(solution)/shard_map/all_gather | solution.py:369
  7.9 104.9 %all-gather.6.cloned.1.call-start = ((), (), s32[]{:S(2)}) async-start(), calls=%async_computation.8 | async-start | bytes 1572864 | tf_op jit(solution)/shard_map/all_gather | solution.py:370
  9.3 166.5 %copy-start.48 = (f32[128]{0:T(128)}, f32[128]{0:T(128)S(1)}, u32[]{:S(2)}) copy-start(f32[128]{0:T(128)S(1)} %compare_convert_fusion) | copy-start | bytes 1540
  74.8 4.8 %copy-start.50 = (s32[128]{0:T(128)S(1)}, s32[128]{0:T(128)}, u32[]{:S(2)}) copy-start(s32[128]{0:T(128)} %param.15) | copy-start | bytes 1540
  75.0 6.3 %copy-start.32 = (f32[1024,1]{0,1:T(1,128)}, f32[1024,1]{0,1:T(1,128)S(1)}, u32[]{:S(2)}) copy-start(f32[1024,1]{0,1:T(1,128)S(1)} %copy.100) | copy-start | bytes 12292
  75.1 6.1 %copy-start.43 = (f32[128]{0:T(128)}, f32[128]{0:T(128)S(1)}, u32[]{:S(2)}) copy-start(f32[128]{0:T(128)S(1)} %add_rsqrt_fusion.1) | copy-start | bytes 1540
  79.6 93.3 %copy-start.42 = (pred[128,128]{0,1:T(8,128)(4,1)}, pred[128,128]{0,1:T(8,128)(4,1)S(1)}, u32[]{:S(2)}) copy-start(pred[128,128]{0,1:T(8,128)(4,1)S(1)} %compare_and_fusion.1) | copy-start | bytes 49156
  81.7 3.6 %copy-start.28 = (bf16[128,8,32]{0,2,1:T(8,128)(2,1)}, bf16[128,8,32]{0,2,1:T(8,128)(2,1)S(1)}, u32[]{:S(2)}) copy-start(bf16[128,8,32]{0,2,1:T(8,128)(2,1)S(1)} %get-tuple-element.80) | copy-start | bytes 196612
  81.7 3.6 %copy-start.30 = (bf16[128,8,32]{0,2,1:T(8,128)(2,1)}, bf16[128,8,32]{0,2,1:T(8,128)(2,1)S(1)}, u32[]{:S(2)}) copy-start(bf16[128,8,32]{0,2,1:T(8,128)(2,1)S(1)} %get-tuple-element.81) | copy-start | bytes 196612
  82.5 3.3 %copy-start.13 = (f32[8,2,128,128]{2,3,1,0:T(8,128)}, f32[8,2,128,128]{2,3,1,0:T(8,128)S(1)}, u32[]{:S(2)}) copy-start(f32[8,2,128,128]{2,3,1,0:T(8,128)S(1)} %fusion.20) | copy-start | bytes 3145732
  83.0 4.0 %copy-start.15 = (bf16[8,64,2,128]{3,1,2,0:T(8,128)(2,1)}, bf16[8,64,2,128]{3,1,2,0:T(8,128)(2,1)S(1)}, u32[]{:S(2)}) copy-start(bf16[8,64,2,128]{3,1,2,0:T(8,128)(2,1)S(1)} %fusion.25) | copy-start | bytes 786436
  85.3 27.4 %copy-start.2 = (f32[128,1024]{1,0:T(8,128)}, f32[128,1024]{1,0:T(8,128)S(1)}, u32[]{:S(2)}) copy-start(f32[128,1024]{1,0:T(8,128)S(1)} %get-tuple-element.89) | copy-start | bytes 1572868
  85.3 27.4 %copy-start.46 = (f32[128]{0:T(128)}, f32[128]{0:T(128)S(1)}, u32[]{:S(2)}) copy-start(f32[128]{0:T(128)S(1)} %add_rsqrt_fusion) | copy-start | bytes 1540
  85.5 27.2 %copy-start.38 = (f32[1024,1]{0,1:T(1,128)}, f32[1024,1]{0,1:T(1,128)S(1)}, u32[]{:S(2)}) copy-start(f32[1024,1]{0,1:T(1,128)S(1)} %copy.101) | copy-start | bytes 12292
  85.7 58.1 %copy-start.36 = (f32[16,128]{1,0:T(8,128)}, f32[16,128]{1,0:T(8,128)S(1)}, u32[]{:S(2)}) copy-start(f32[16,128]{1,0:T(8,128)S(1)} %get-tuple-element.86) | copy-start | bytes 24580
  85.7 101.4 %copy-start.26 = (f32[128,16]{0,1:T(8,128)}, f32[128,16]{0,1:T(8,128)S(1)}, u32[]{:S(2)}) copy-start(f32[128,16]{0,1:T(8,128)S(1)} %get-tuple-element.87) | copy-start | bytes 24580
  87.1 23.9 %all-to-all-start = ((bf16[16,24,1024]{2,1,0:T(8,128)(2,1)}), bf16[16,24,1024]{2,1,0:T(8,128)(2,1)S(1)}, u32[]{:S(2)}, u32[]{:S(2)}) async-start(bf16[16,24,1024]{2,1,0:T(8,128)(2,1)} %convolution_convert_fusion.8), calls=%async_computation | async-start | bytes 1572864 | tf_op jit(solution)/shard_map/all_to_all | solution.py:409
  92.3 24.1 %all-gather.8.cloned.1.call-start = ((), (), s32[]{:S(2)}) async-start(), calls=%async_computation.9 | async-start | bytes 1572864 | tf_op jit(solution)/shard_map/all_gather | solution.py:371
  116.3 27.4 %copy-start.24 = (bf16[384,512]{1,0:T(8,128)(2,1)}, bf16[384,512]{1,0:T(8,128)(2,1)S(1)}, u32[]{:S(2)}) copy-start(bf16[384,512]{1,0:T(8,128)(2,1)S(1)} %get-tuple-element.90) | copy-start | bytes 1179652
  116.3 27.0 %copy-start.11 = (bf16[128,1024]{1,0:T(8,128)(2,1)S(1)}, bf16[128,1024]{1,0:T(8,128)(2,1)}, u32[]{:S(2)}) copy-start(bf16[128,1024]{1,0:T(8,128)(2,1)} %param.17) | copy-start | bytes 786436
  119.2 24.1 %all-to-all-start.1 = ((bf16[16,24,1024]{2,1,0:T(8,128)(2,1)}), bf16[16,24,1024]{2,1,0:T(8,128)(2,1)S(1)}, u32[]{:S(2)}, u32[]{:S(2)}) async-start(bf16[16,24,1024]{2,1,0:T(8,128)(2,1)} %bitcast.23), calls=%async_computation.1 | async-start | bytes 1572864 | tf_op jit(solution)/shard_map/all_to_all | solution.py:412
  124.6 166.6 %reduce-scatter.4.cloned.1.call-start = ((), (), s32[]{:S(2)}) async-start(), calls=%async_computation.10 | async-start | bytes 1572864 | tf_op jit(solution)/shard_map/reduce_scatter | solution.py:529
  143.3 26.1 %copy-start.17 = (f32[384,512]{1,0:T(8,128)S(1)}, f32[384,512]{1,0:T(8,128)}, u32[]{:S(2)}) copy-start(f32[384,512]{1,0:T(8,128)} %copy-done.16) | copy-start | bytes 2359300
  143.3 26.1 %copy-start.51 = (bf16[1,512,1024]{2,1,0:T(8,128)(2,1)S(1)}, bf16[1,512,1024]{2,1,0:T(8,128)(2,1)}, u32[]{:S(2)}) copy-start(bf16[1,512,1024]{2,1,0:T(8,128)(2,1)} %all-gather.8.cloned.1.call-done) | copy-start | bytes 3145732
  143.3 26.1 %copy-start.52 = (f32[384,512]{1,0:T(8,128)S(1)}, f32[384,512]{1,0:T(8,128)}, u32[]{:S(2)}) copy-start(f32[384,512]{1,0:T(8,128)} %get-tuple-element.91) | copy-start | bytes 2359300
  172.8 6.4 %copy-start.5 = (bf16[1,1024,512]{2,1,0:T(8,128)(2,1)S(1)}, bf16[1,1024,512]{2,1,0:T(8,128)(2,1)}, u32[]{:S(2)}) copy-start(bf16[1,1024,512]{2,1,0:T(8,128)(2,1)} %all-gather.4.cloned.1.call-done) | copy-start | bytes 3145732
  172.9 120.5 %reduce-scatter.6.cloned.1.call-start = ((), (), s32[]{:S(2)}) async-start(), calls=%async_computation.11 | async-start | bytes 1572864 | tf_op jit(solution)/shard_map/reduce_scatter | solution.py:532
  182.5 23.0 %all-to-all-start.3 = ((bf16[16,24,1024]{2,1,0:T(8,128)(2,1)}), bf16[16,24,1024]{2,1,0:T(8,128)(2,1)}, u32[]{:S(2)}, u32[]{:S(2)}) async-start(bf16[16,24,1024]{2,1,0:T(8,128)(2,1)} %bitcast.30), calls=%async_computation.3 | async-start | bytes 1572864 | tf_op jit(solution)/shard_map/all_to_all | solution.py:440
  186.8 108.7 %reduce-scatter.8.cloned.1.call-start = ((), (), s32[]{:S(2)}) async-start(), calls=%async_computation.12 | async-start | bytes 1572864 | tf_op jit(solution)/shard_map/reduce_scatter | solution.py:535
  193.9 4.8 %copy-start.7 = (bf16[16,24,1024]{2,1,0:T(8,128)(2,1)S(1)}, bf16[16,24,1024]{2,1,0:T(8,128)(2,1)}, u32[]{:S(2)}) copy-start(bf16[16,24,1024]{2,1,0:T(8,128)(2,1)} %copy-done.6) | copy-start | bytes 2359300
  193.9 4.8 %copy-start.25 = (bf16[384,512]{1,0:T(8,128)(2,1)S(1)}, bf16[384,512]{1,0:T(8,128)(2,1)}, u32[]{:S(2)}) copy-start(bf16[384,512]{1,0:T(8,128)(2,1)} %copy-done.24) | copy-start | bytes 1179652
  195.5 10.0 %copy-start.27 = (f32[128,16]{0,1:T(8,128)S(1)}, f32[128,16]{0,1:T(8,128)}, u32[]{:S(2)}) copy-start(f32[128,16]{0,1:T(8,128)} %copy-done.26) | copy-start | bytes 24580
  195.5 10.0 %copy-start.37 = (f32[16,128]{1,0:T(8,128)S(1)}, f32[16,128]{1,0:T(8,128)}, u32[]{:S(2)}) copy-start(f32[16,128]{1,0:T(8,128)} %copy-done.36) | copy-start | bytes 24580
  195.5 11.7 %copy-start.3 = (f32[128,1024]{1,0:T(8,128)S(1)}, f32[128,1024]{1,0:T(8,128)}, u32[]{:S(2)}) copy-start(f32[128,1024]{1,0:T(8,128)} %copy-done.2) | copy-start | bytes 1572868
  195.5 11.7 %copy-start.39 = (f32[1024,1]{0,1:T(1,128)S(1)}, f32[1024,1]{0,1:T(1,128)}, u32[]{:S(2)}) copy-start(f32[1024,1]{0,1:T(1,128)} %copy-done.38) | copy-start | bytes 12292
  195.5 11.7 %copy-start.40 = (bf16[128,16]{0,1:T(8,128)(2,1)S(1)}, bf16[128,16]{0,1:T(8,128)(2,1)}, u32[]{:S(2)}) copy-start(bf16[128,16]{0,1:T(8,128)(2,1)} %get-tuple-element.82) | copy-start | bytes 12292
  195.5 11.7 %copy-start.47 = (f32[128]{0:T(128)S(1)}, f32[128]{0:T(128)}, u32[]{:S(2)}) copy-start(f32[128]{0:T(128)} %copy-done.46) | copy-start | bytes 1540
  198.8 9.8 %copy-start.8 = (f32[128,1024]{1,0:T(8,128)S(1)}, f32[128,1024]{1,0:T(8,128)}, u32[]{:S(2)}) copy-start(f32[128,1024]{1,0:T(8,128)} %multiply_reduce_fusion) | copy-start | bytes 1572868
  198.8 9.8 %copy-start.12 = (bf16[128,1024]{1,0:T(8,128)(2,1)S(1)}, bf16[128,1024]{1,0:T(8,128)(2,1)}, u32[]{:S(2)}) copy-start(bf16[128,1024]{1,0:T(8,128)(2,1)} %param.17) | copy-start | bytes 786436
  205.5 4.0 %copy-start.1 = (bf16[32,32,1536]{2,1,0:T(8,128)(2,1)S(1)}, bf16[32,32,1536]{2,1,0:T(8,128)(2,1)}, u32[]{:S(2)}) copy-start(bf16[32,32,1536]{2,1,0:T(8,128)(2,1)} %get-tuple-element.17) | copy-start | bytes 9437188
  209.5 3.2 %copy-start.21 = (bf16[128,8,2,32]{0,3,2,1:T(8,128)(2,1)S(1)}, bf16[128,8,2,32]{0,3,2,1:T(8,128)(2,1)}, u32[]{:S(2)}) copy-start(bf16[128,8,2,32]{0,3,2,1:T(8,128)(2,1)} %copy-done.20) | copy-start | bytes 393220
  210.4 6.4 %copy-start.23 = (f32[128,32]{0,1:T(8,128)S(1)}, f32[128,32]{0,1:T(8,128)}, u32[]{:S(2)}) copy-start(f32[128,32]{0,1:T(8,128)} %copy-done.22) | copy-start | bytes 49156
  214.7 4.7 %copy-start.33 = (f32[1024,1]{0,1:T(1,128)S(1)}, f32[1024,1]{0,1:T(1,128)}, u32[]{:S(2)}) copy-start(f32[1024,1]{0,1:T(1,128)} %copy-done.32) | copy-start | bytes 12292
  214.7 4.7 %copy-start.44 = (f32[128]{0:T(128)S(1)}, f32[128]{0:T(128)}, u32[]{:S(2)}) copy-start(f32[128]{0:T(128)} %copy-done.43) | copy-start | bytes 1540
  219.4 5.0 %copy-start.35 = (bf16[1024,16]{0,1:T(8,128)(2,1)S(1)}, bf16[1024,16]{0,1:T(8,128)(2,1)}, u32[]{:S(2)}) copy-start(bf16[1024,16]{0,1:T(8,128)(2,1)} %convolution_convert_fusion.10) | copy-start | bytes 98308
  225.7 3.7 %copy-start.34 = (f32[1024,1]{0,1:T(1,128)S(1)}, f32[1024,1]{0,1:T(1,128)}, u32[]{:S(2)}) copy-start(f32[1024,1]{0,1:T(1,128)} %copy-done.32) | copy-start | bytes 12292
  225.7 3.7 %copy-start.45 = (f32[128]{0:T(128)S(1)}, f32[128]{0:T(128)}, u32[]{:S(2)}) copy-start(f32[128]{0:T(128)} %copy-done.43) | copy-start | bytes 1540
  (14 other events, 23.2 us)
Sparse Core Ops, SparseCore 0:
  9.5 24.5 all-gather.3
  35.7 35.7 all-gather.5
  94.6 21.6 all-gather.7
  173.0 18.7 reduce-scatter.3
  193.8 20.3 reduce-scatter.5
  216.4 20.3 reduce-scatter.7
where the time goes:
time: 306 us; the launch traced here: 304 us
  Pallas kernels  105 us (34%)
  matrix products  53.6 us (18%)
  waiting for transfers between devices  42.4 us (14%)
  other arithmetic  26.4 us (9%)
  blocking collectives  25.3 us (8%)
  local copies, waits for them, and re-layouts  21.6 us (7%)
  starting transfers between devices  15.3 us (5%)
  between operations  15 us (5%)
    pallas_call x1, Pallas kernels, gather_rows(): pl.pallas_call(lambda *refs: gather_kernel(sizes, *refs), out_shape=tuple...  58 us
    pallas_call x1, Pallas kernels, scatter_rows(): pl.pallas_call(lambda *refs: scatter_kernel(sizes, *refs), out_shape=tupl...  46.8 us
    all_to_all x1, blocking collectives, shards(): lax.all_to_all(grad_send, 'dp', split_axis=0, concat_axis=0, tiled=True)  25.3 us
    all_to_all x1, waiting for transfers between devices, shards(): lax.all_to_all(send_rows, 'dp', split_axis=0, concat_axis=0, tiled=True)  17.9 us
    all_to_all x1, waiting for transfers between devices, shards(): lax.all_to_all(out_rows.reshape(recv_rows.shape), 'dp', split_axis=0, con...  17.4 us
    convert_element_type x3, other arithmetic, shards(): expert_grads = (lax.psum_scatter(grad_gate_w[None].astype(jnp.bfloat16),...  6.42 us
  transfers between devices with their start and end apart: 9, of which 3 were waited for; matrix products, arithmetic and copies ran while one was open for 30% of the time, Pallas kernels for 34%

commit v1 on v0

v1 whole, which is shorter than its diff:
```python
import functools

import jax
import jax.numpy as jnp
from jax import lax
from jax.experimental import pallas as pl
from jax.experimental.pallas import tpu as pltpu
from jax.sharding import PartitionSpec as P

HEADS = 16
KV_HEADS = 8
HEAD_DIM = 64
TOP = 8
CAP = 24


norm_eps = 1e-05


def positions_mask(doc_block):
    row_count = doc_block.shape[0]
    row_index = jnp.arange(row_count)
    same_doc = doc_block[:, None] == doc_block[None, :]
    earlier = row_index[None, :] < row_index[:, None]
    position = jnp.sum((same_doc & earlier).astype(jnp.float32), axis=1)
    allowed = same_doc & (row_index[None, :] <= row_index[:, None])
    live_rows = (doc_block < row_count).astype(jnp.float32)
    return (position, allowed, live_rows)


def rope_tables(position):
    half_dim = HEAD_DIM // 2
    freqs = jnp.exp(-jnp.log(10000.0) * (2.0 * jnp.arange(half_dim, dtype=jnp.float32) / HEAD_DIM))
    angle = position[:, None] * freqs[None, :]
    return (jnp.cos(angle), jnp.sin(angle))


def rotate(values, cosine, sinusoid):
    half_dim = values.shape[-1] // 2
    first_half, second_half = (values[..., :half_dim], values[..., half_dim:])
    return jnp.concatenate(
        [
            first_half * cosine - second_half * sinusoid,
            second_half * cosine + first_half * sinusoid,
        ],
        axis=-1,
    )


def unrotate(values, cosine, sinusoid):
    half_dim = values.shape[-1] // 2
    first_half, second_half = (values[..., :half_dim], values[..., half_dim:])
    return jnp.concatenate(
        [
            first_half * cosine + second_half * sinusoid,
            second_half * cosine - first_half * sinusoid,
        ],
        axis=-1,
    )


def norm_forward(values, gain):
    scale_row = lax.rsqrt(jnp.mean(values * values, axis=-1, keepdims=True) + norm_eps)
    normed = values * scale_row
    return (normed, scale_row, (normed * gain).astype(jnp.bfloat16))


def norm_backward(upstream, normed, scale_row, gain):
    scaled = upstream * gain
    inner = jnp.mean(scaled * normed, axis=-1, keepdims=True)
    return (scale_row * (scaled - normed * inner), jnp.sum(upstream * normed, axis=0))


def probabilities(query_b, key_b, allowed, log_total):
    scores = jnp.einsum(
        "ikgd,jkd->kgij", query_b, key_b, preferred_element_type=jnp.float32
    ) * HEAD_DIM ** (-0.5)
    raised = jnp.where(allowed[None, None], jnp.exp(scores), 0.0)
    if log_total is None:
        log_total = jnp.log(jnp.sum(raised, axis=-1, keepdims=True))
    return (jnp.where(allowed[None, None], jnp.exp(scores - log_total), 0.0), log_total)


def slots_of(expert_block, live_rows, experts):
    row_count = expert_block.shape[0]
    chosen = jnp.sum(
        (expert_block[:, :, None] == jnp.arange(experts)[None, None, :]).astype(jnp.float32), axis=1
    )
    member = chosen * live_rows[:, None]
    lower = (jnp.arange(row_count)[None, :] < jnp.arange(row_count)[:, None]).astype(jnp.bfloat16)
    rank = jnp.dot(lower, member.astype(jnp.bfloat16), preferred_element_type=jnp.float32)
    kept = member * (rank < CAP).astype(jnp.float32)
    slot_match = (rank.T[:, None, :] == jnp.arange(CAP, dtype=jnp.float32)[None, :, None]).astype(
        jnp.float32
    )
    dispatch = kept.T[:, None, :] * slot_match
    return (dispatch, kept, chosen, rank)


def split_bf16(values):
    high = values.astype(jnp.bfloat16)
    left = values - lax.reduce_precision(values, 8, 7)
    middle = left.astype(jnp.bfloat16)
    low = (left - lax.reduce_precision(left, 8, 7)).astype(jnp.bfloat16)
    return (high, middle, low)


def expert_forward(rows_in, w_gate, w_up, w_down):
    gate_pre = jnp.dot(rows_in, w_gate, preferred_element_type=jnp.float32)
    up_pre = jnp.dot(rows_in, w_up, preferred_element_type=jnp.float32)
    act_rows = (jax.nn.silu(gate_pre) * up_pre).astype(jnp.bfloat16)
    out_rows = jnp.dot(act_rows, w_down, preferred_element_type=jnp.float32).astype(jnp.bfloat16)
    return (gate_pre, up_pre, act_rows, out_rows)


def expert_backward(rows_in, gate_pre, up_pre, act_rows, grad_rows, w_gate, w_up, w_down):
    grad_act = jnp.dot(grad_rows, w_down.T, preferred_element_type=jnp.float32)
    sigmoid_gate = jax.nn.sigmoid(gate_pre)
    grad_up_pre = (grad_act * gate_pre * sigmoid_gate).astype(jnp.bfloat16)
    grad_gate_pre = (
        grad_act * up_pre * sigmoid_gate * (1.0 + gate_pre * (1.0 - sigmoid_gate))
    ).astype(jnp.bfloat16)
    grad_down_w = jnp.dot(act_rows.T, grad_rows, preferred_element_type=jnp.float32)
    grad_gate_w = jnp.dot(rows_in.T, grad_gate_pre, preferred_element_type=jnp.float32)
    grad_up_w = jnp.dot(rows_in.T, grad_up_pre, preferred_element_type=jnp.float32)
    grad_rows_in = jnp.dot(grad_gate_pre, w_gate.T, preferred_element_type=jnp.float32)
    grad_rows_in = (
        grad_rows_in + jnp.dot(grad_up_pre, w_up.T, preferred_element_type=jnp.float32)
    ).astype(jnp.bfloat16)
    return (grad_rows_in, grad_gate_w, grad_up_w, grad_down_w)


def axis_bits(size):
    return size.bit_length() - 1


def span(bits):
    masks = [0]
    for bit in bits:
        masks = masks + [mask | (1 << bit) for mask in masks]
    return masks


def dimension_bits(sizes):
    dp_bits, fsdp_bits = (axis_bits(sizes[0]), axis_bits(sizes[1]))
    x_bits = list(range(fsdp_bits))
    high = [fsdp_bits + bit for bit in range(dp_bits - 1, 0, -1)]
    return {"x": x_bits, "z": high[:-1], "y": high[-1:], "c": [fsdp_bits] if dp_bits else []}


def bit_order(sizes, letters):
    bits = dimension_bits(sizes)
    return [bit for letter in letters for bit in bits[letter]]


class Cube:
    def __init__(self, sizes):
        self.sizes = sizes
        self.dp = lax.axis_index("dp")
        self.fsdp = lax.axis_index("fsdp")
        self.me = self.dp * sizes[1] + self.fsdp
        self.fsdp_bits = axis_bits(sizes[1])
        self.bits = axis_bits(sizes[0]) + self.fsdp_bits
        self.flips = [
            (1 - 2 * ((self.me // (1 << bit)) % 2)) * (1 << bit) for bit in range(self.bits)
        ]

    def block(self, mask):
        index = self.me
        for bit, flip in enumerate(self.flips):
            if mask >> bit & 1:
                index = index + flip
        return index

    def device(self, mask):
        other = self.block(mask)
        return {"dp": other // self.sizes[1], "fsdp": other % self.sizes[1]}

    def dp_masks(self):
        masks = [part << self.fsdp_bits for part in range(1, self.sizes[0])]
        return sorted(masks, reverse=True)

    def fsdp_masks(self):
        return list(range(1, self.sizes[1]))

    def greet(self, masks):
        barrier = pltpu.get_barrier_semaphore()
        for mask in masks:
            pl.semaphore_signal(
                barrier, inc=1, device_id=self.device(mask), device_id_type=pl.DeviceIdType.MESH
            )
        pl.semaphore_wait(barrier, len(masks))

    def send(self, source, target, send_sem, recv_sem, mask):
        copy = pltpu.make_async_remote_copy(
            src_ref=source,
            dst_ref=target,
            send_sem=send_sem,
            recv_sem=recv_sem,
            device_id=self.device(mask),
            device_id_type=pl.DeviceIdType.MESH,
        )
        copy.start()
        return copy


def link_time(sizes, bit, volume):
    return volume / (8.0 if bit in dimension_bits(sizes)["c"] else 1.0)


def gather_plan(sizes, orders, volumes):
    free = {}
    known = [{0: 0.0} for _ in orders]
    waiting = []
    for which, order in enumerate(orders):
        for stage, bit in enumerate(order):
            for mask in span(order[:stage]):
                waiting.append((which, mask, bit, len(order) - stage))
    plan = []
    while waiting:
        best = None
        for item in waiting:
            which, mask, bit, left = item
            if mask not in known[which]:
                continue
            begin = max(known[which][mask], free.get(bit, 0.0))
            rank = (begin, -left, which, mask)
            if best is None or rank < best[0]:
                best = (rank, item)
        (begin, _, _, _), item = best
        which, mask, bit, _ = item
        end = begin + link_time(sizes, bit, volumes[which])
        free[bit] = end
        known[which][mask | (1 << bit)] = end + 0.3 * min(volumes)
        plan.append((which, mask, bit))
        waiting.remove(item)
    return plan


def scatter_plan(sizes, orders, volumes):
    free = {}
    known = [{} for _ in orders]
    waiting = []
    for which, order in enumerate(orders):
        for stage, bit in enumerate(order):
            for rest in span(order[stage + 1 :]):
                waiting.append((which, stage, rest | (1 << bit)))
    plan = []
    while waiting:
        best = None
        for item in waiting:
            which, stage, mask = item
            needs = [mask | (1 << earlier) for earlier in orders[which][:stage]]
            if any(need not in known[which] for need in needs):
                continue
            bit = orders[which][stage]
            ready = max([known[which][need] for need in needs], default=0.0)
            begin = max(ready, free.get(bit, 0.0))
            after = [at for at, later in enumerate(orders[which]) if mask >> later & 1 and at > stage]
            rank = (begin, after[0] if after else len(orders[which]), which, mask)
            if best is None or rank < best[0]:
                best = (rank, item)
        rank, item = best
        which, stage, mask = item
        bit = orders[which][stage]
        end = rank[0] + link_time(sizes, bit, volumes[which])
        free[bit] = end
        known[which][mask] = end + 0.3 * min(volumes)
        plan.append(item)
        waiting.remove(item)
    return plan


def volume_of(shape):
    total = 1
    for size in shape:
        total = total * size
    return total


GATHER_ORDERS = ("xzyc", "xzyc", "xzyc", "zxyc", "xzyc")
SCATTER_ORDERS = ("zyxc", "xyzc", "zyxc", "zxyc", "zxyc")


def front_kernel(sizes, count, *refs):
    shards, experts, rows = (refs[:count], refs[count : count + 3], refs[count + 3])
    outs = refs[count + 4 :]
    full, wide, rows_out = (outs[:count], outs[count : count + 3], outs[count + 3])
    local_sems, send_sems, recv_sems, wide_send, wide_recv, row_send, row_recv = outs[count + 4 :]
    cube = Cube(sizes)
    singles = [1 << bit for bit in range(cube.bits)]
    cube.greet(sorted(set(singles + cube.dp_masks() + cube.fsdp_masks())))
    own = []
    for which, (source, target) in enumerate(zip(shards, full)):
        own.append((source, target.at[cube.me]))
    for which, (source, target) in enumerate(zip(experts, wide)):
        own.append((source, target.at[cube.fsdp]))
    own.append((rows.at[cube.dp], rows_out.at[cube.dp]))
    pending = []
    for mask in cube.fsdp_masks():
        for which, (source, target) in enumerate(zip(experts, wide)):
            pending.append(
                cube.send(
                    source,
                    target.at[cube.fsdp],
                    wide_send.at[which, mask],
                    wide_recv.at[which, mask],
                    mask,
                )
            )
    orders = [bit_order(sizes, letters) for letters in GATHER_ORDERS]
    plan = gather_plan(sizes, orders, [volume_of(ref.shape) for ref in shards])
    copies = [{} for _ in shards]
    arrived = [{0} for _ in shards]
    started = False
    for which, mask, bit in plan:
        if mask and not started:
            started = True
            for peer in cube.dp_masks():
                part = peer >> cube.fsdp_bits
                pending.append(
                    cube.send(
                        rows.at[cube.block(peer) // sizes[1]],
                        rows_out.at[cube.dp],
                        row_send.at[part],
                        row_recv.at[part],
                        peer,
                    )
                )
            for at, (source, target) in enumerate(own):
                own[at] = pltpu.make_async_copy(source, target, local_sems.at[at])
                own[at].start()
        if mask not in arrived[which]:
            copies[which][mask].wait_recv()
            arrived[which].add(mask)
        label = mask | (1 << bit)
        target = full[which]
        copies[which][label] = cube.send(
            target.at[cube.block(mask)] if mask else shards[which],
            target.at[cube.block(mask)],
            send_sems.at[which, label],
            recv_sems.at[which, label],
            1 << bit,
        )
    for which, made in enumerate(copies):
        for label, copy in made.items():
            if label not in arrived[which]:
                copy.wait_recv()
    for copy in pending:
        copy.wait_recv()
    for copy in own:
        copy.wait()
    for made in copies:
        for copy in made.values():
            copy.wait_send()
    for copy in pending:
        copy.wait_send()


def front_gather(sizes, shards, experts, rows):
    blocks = sizes[0] * sizes[1]
    count = len(shards)
    out_shape = [jax.ShapeDtypeStruct((blocks,) + part.shape, part.dtype) for part in shards]
    out_shape += [jax.ShapeDtypeStruct((sizes[1],) + part.shape, part.dtype) for part in experts]
    out_shape += [jax.ShapeDtypeStruct(rows.shape, rows.dtype)]
    dma = pltpu.SemaphoreType.DMA
    return pl.pallas_call(
        lambda *refs: front_kernel(sizes, count, *refs),
        out_shape=tuple(out_shape),
        in_specs=[pl.BlockSpec(memory_space=pltpu.VMEM)] * (count + 4),
        out_specs=(pl.BlockSpec(memory_space=pl.ANY),) * (count + 4),
        scratch_shapes=[
            dma((count + 4,)),
            dma((count, blocks)),
            dma((count, blocks)),
            dma((3, sizes[1])),
            dma((3, sizes[1])),
            dma((sizes[0],)),
            dma((sizes[0],)),
        ],
        compiler_params=pltpu.CompilerParams(
            collective_id=0, has_side_effects=True, vmem_limit_bytes=24 * 1024 * 1024
        ),
        name="front_gather",
    )(*shards, *experts, rows)


def swap_kernel(sizes, count, parts, *refs):
    rows, grads = (refs[:count], refs[count : count + parts])
    outs = refs[count + parts :]
    rows_out, grads_out = (outs[:count], outs[count : count + parts])
    local_sems, row_send, row_recv, part_send, part_recv = outs[count + parts :]
    cube = Cube(sizes)
    cube.greet(cube.dp_masks() + (cube.fsdp_masks() if parts else []))
    pending = []
    for peer in cube.dp_masks():
        part = peer >> cube.fsdp_bits
        for which in range(count):
            pending.append(
                cube.send(
                    rows[which].at[cube.block(peer) // sizes[1]],
                    rows_out[which].at[cube.dp],
                    row_send.at[which, part],
                    row_recv.at[which, part],
                    peer,
                )
            )
    for mask in cube.fsdp_masks() if parts else []:
        for which in range(parts):
            pending.append(
                cube.send(
                    grads[which].at[cube.block(mask) % sizes[1]],
                    grads_out[which].at[mask - 1],
                    part_send.at[which, mask],
                    part_recv.at[which, mask],
                    mask,
                )
            )
    own = []
    for which in range(count):
        own.append(
            pltpu.make_async_copy(
                rows[which].at[cube.dp], rows_out[which].at[cube.dp], local_sems.at[which]
            )
        )
        own[-1].start()
    for copy in pending:
        copy.wait_recv()
    for copy in own:
        copy.wait()
    for copy in pending:
        copy.wait_send()


def swap_rows(sizes, rows, grads, collective_id, name):
    count, parts = (len(rows), len(grads))
    peers = max(sizes[1] - 1, 1)
    out_shape = [jax.ShapeDtypeStruct(part.shape, part.dtype) for part in rows]
    out_shape += [
        jax.ShapeDtypeStruct((peers,) + part.shape[1:], part.dtype) for part in grads
    ]
    dma = pltpu.SemaphoreType.DMA
    return pl.pallas_call(
        lambda *refs: swap_kernel(sizes, count, parts, *refs),
        out_shape=tuple(out_shape),
        in_specs=[pl.BlockSpec(memory_space=pltpu.VMEM)] * (count + parts),
        out_specs=(pl.BlockSpec(memory_space=pl.ANY),) * (count + parts),
        scratch_shapes=[
            dma((count,)),
            dma((count, sizes[0])),
            dma((count, sizes[0])),
            dma((max(parts, 1), sizes[1])),
            dma((max(parts, 1), sizes[1])),
        ],
        compiler_params=pltpu.CompilerParams(
            collective_id=collective_id,
            has_side_effects=True,
            vmem_limit_bytes=24 * 1024 * 1024,
        ),
        name=name,
    )(*rows, *grads)


def scatter_kernel(sizes, count, *refs):
    sources, outs = (refs[:count], refs[count : 2 * count])
    slots, held = (refs[2 * count : 3 * count], refs[3 * count : 4 * count])
    send_sems, recv_sems = refs[4 * count :]
    cube = Cube(sizes)
    cube.greet([1 << bit for bit in range(cube.bits)])
    orders = [bit_order(sizes, letters)[::-1] for letters in SCATTER_ORDERS]
    copies = [{} for _ in sources]
    arrived = [set() for _ in sources]
    places = [{} for _ in sources]

    def total(which, mask, stage):
        value = sources[which][cube.block(mask)].astype(jnp.float32)
        for earlier in orders[which][:stage]:
            label = mask | (1 << earlier)
            copies[which][label].wait_recv()
            value = value + slots[which][label].astype(jnp.float32)
        return value

    for which, stage, mask in scatter_plan(
        sizes, orders, [volume_of(ref.shape) for ref in outs]
    ):
        if stage == 0:
            leaving = sources[which].at[cube.block(mask)]
        else:
            slot = places[which].setdefault(mask, len(places[which]))
            held[which][slot] = total(which, mask, stage).astype(jnp.bfloat16)
            leaving = held[which].at[slot]
        copies[which][mask] = cube.send(
            leaving,
            slots[which].at[mask],
            send_sems.at[which, mask],
            recv_sems.at[which, mask],
            1 << orders[which][stage],
        )
    for which in range(count):
        outs[which][...] = total(which, 0, len(orders[which]))
    for made in copies:
        for copy in made.values():
            copy.wait_send()


def scatter_rows(sizes, packed):
    blocks = sizes[0] * sizes[1]
    count = len(packed)
    shapes = [part.shape[1:] for part in packed]
    dma = pltpu.SemaphoreType.DMA
    return pl.pallas_call(
        lambda *refs: scatter_kernel(sizes, count, *refs),
        out_shape=tuple(jax.ShapeDtypeStruct(shape, jnp.float32) for shape in shapes),
        in_specs=[pl.BlockSpec(memory_space=pltpu.VMEM)] * count,
        out_specs=(pl.BlockSpec(memory_space=pltpu.VMEM),) * count,
        scratch_shapes=[pltpu.VMEM((blocks,) + shape, jnp.bfloat16) for shape in shapes]
        + [pltpu.VMEM((blocks // 2,) + shape, jnp.bfloat16) for shape in shapes]
        + [dma((count, blocks)), dma((count, blocks))],
        compiler_params=pltpu.CompilerParams(
            collective_id=3, has_side_effects=True, vmem_limit_bytes=48 * 1024 * 1024
        ),
        name="scatter_rows",
    )(*packed)


def shards(
    sizes,
    hidden_in,
    doc_id,
    expert_ids,
    out_grad,
    attn_gain,
    query_weight,
    key_weight,
    value_weight,
    output_weight,
    ffn_gain,
    router_weight,
    expert_gate,
    expert_up,
    expert_down,
):
    rows = hidden_in.shape[0]
    groups = HEADS // KV_HEADS
    scale = HEAD_DIM ** (-0.5)
    experts_all = router_weight.shape[1]
    query_width, key_width = (query_weight.shape[1], key_weight.shape[1])
    small_width = -(-(experts_all + 2) // 128) * 128
    small = jnp.concatenate([router_weight, attn_gain[:, None], ffn_gain[:, None]], axis=1)
    small = jnp.pad(small, ((0, 0), (0, small_width - small.shape[1])))
    position, allowed, live_rows = positions_mask(doc_id)
    dispatch, kept, chosen, rank = slots_of(expert_ids, live_rows, experts_all)
    dispatch_b = dispatch.astype(jnp.bfloat16)
    pulled_b = jnp.einsum(
        "ecr,rd->ecd", dispatch_b, out_grad, preferred_element_type=jnp.float32
    ).astype(jnp.bfloat16)
    gathered = front_gather(
        sizes,
        (query_weight, key_weight, value_weight, output_weight, small),
        (expert_gate[0], expert_up[0], expert_down[0]),
        pulled_b,
    )
    w_query, w_key, w_value, w_output, full_small = [
        part.reshape(-1, part.shape[2]) for part in gathered[:5]
    ]
    w_router = full_small[:, :experts_all]
    gain_one, gain_two = (full_small[:, experts_all], full_small[:, experts_all + 1])
    w_gate, w_up, w_down = [part.reshape(-1, part.shape[2]) for part in gathered[5:8]]
    grad_recv = gathered[8]
    cosine, sinusoid = rope_tables(position)
    cos_query, sin_query = (cosine[:, None, None, :], sinusoid[:, None, None, :])
    cos_key, sin_key = (cosine[:, None, :], sinusoid[:, None, :])
    resid_in = hidden_in.astype(jnp.float32)
    normed_one, scale_one, normed_in = norm_forward(resid_in, gain_one.astype(jnp.float32))
    query_raw = jnp.dot(normed_in, w_query, preferred_element_type=jnp.float32).reshape(
        rows, KV_HEADS, groups, HEAD_DIM
    )
    key_raw = jnp.dot(normed_in, w_key, preferred_element_type=jnp.float32).reshape(
        rows, KV_HEADS, HEAD_DIM
    )
    query_b = rotate(query_raw, cos_query, sin_query).astype(jnp.bfloat16)
    key_b = rotate(key_raw, cos_key, sin_key).astype(jnp.bfloat16)
    value_b = (
        jnp.dot(normed_in, w_value, preferred_element_type=jnp.float32)
        .reshape(rows, KV_HEADS, HEAD_DIM)
        .astype(jnp.bfloat16)
    )
    probs, log_total = probabilities(query_b, key_b, allowed, None)
    probs_b = probs.astype(jnp.bfloat16)
    mixed = jnp.einsum("kgij,jkd->ikgd", probs_b, value_b, preferred_element_type=jnp.float32)
    mixed_b = (
        (mixed * live_rows[:, None, None, None])
        .reshape(rows, HEADS * HEAD_DIM)
        .astype(jnp.bfloat16)
    )
    resid_mid = resid_in + jnp.dot(mixed_b, w_output, preferred_element_type=jnp.float32)
    normed_two, scale_two, routed_in = norm_forward(resid_mid, gain_two.astype(jnp.float32))
    logits = jnp.dot(routed_in, w_router, preferred_element_type=jnp.float32)
    raised = jnp.where(chosen > 0, jnp.exp(logits), 0.0)
    gates = raised / jnp.sum(raised, axis=1, keepdims=True)
    send_rows = jnp.einsum(
        "ecr,rd->ecd", dispatch_b, routed_in, preferred_element_type=jnp.float32
    ).astype(jnp.bfloat16)
    combine = dispatch * gates.T[:, None, :]
    slot_gate = jnp.sum(combine, axis=2, keepdims=True)
    pieces = split_bf16(slot_gate)
    lanes = jnp.arange(128)[None, None, :]
    packed_gate = sum(
        jnp.where(lanes == at, piece, jnp.zeros((), jnp.bfloat16)) for at, piece in enumerate(pieces)
    )
    (recv,) = swap_rows(
        sizes, (jnp.concatenate([send_rows, packed_gate], axis=2),), (), 1, "swap_out"
    )
    flat = recv.reshape(-1, recv.shape[2])
    width = routed_in.shape[1]
    flat_in = flat[:, :width]
    flat_gate = jnp.sum(flat[:, width : width + 3].astype(jnp.float32), axis=1, keepdims=True)
    gate_pre, up_pre, act_rows, out_rows = expert_forward(flat_in, w_gate, w_up, w_down)
    flat_grad = (flat_gate * grad_recv.reshape(flat_in.shape).astype(jnp.float32)).astype(
        jnp.bfloat16
    )
    grad_rows_in, grad_gate_w, grad_up_w, grad_down_w = expert_backward(
        flat_in, gate_pre, up_pre, act_rows, flat_grad, w_gate, w_up, w_down
    )
    expert_sums = [
        part.reshape((sizes[1], -1) + part.shape[1:])
        for part in (grad_gate_w, grad_up_w, grad_down_w)
    ]
    shape_rows = send_rows.shape
    swapped = swap_rows(
        sizes,
        (out_rows.reshape(shape_rows), grad_rows_in.reshape(shape_rows)),
        [part.astype(jnp.bfloat16) for part in expert_sums],
        2,
        "swap_back",
    )
    back_rows, grad_back = swapped[:2]
    own = lax.axis_index("fsdp")
    expert_grads = [
        lax.dynamic_index_in_dim(mine, own, axis=0, keepdims=True)
        + jnp.sum(other.astype(jnp.float32), axis=0, keepdims=True)
        for mine, other in zip(expert_sums, swapped[2:])
    ]
    expert_sum = sum(
        jnp.einsum("ecr,ecd->rd", piece, back_rows, preferred_element_type=jnp.float32)
        for piece in split_bf16(combine)[:2]
    )
    layer_out = (resid_mid + expert_sum).astype(jnp.bfloat16)
    grad_out = out_grad.astype(jnp.float32)
    slot_dot = jnp.sum(back_rows.astype(jnp.float32) * pulled_b.astype(jnp.float32), axis=2)
    grad_gates = jnp.sum(dispatch * slot_dot[:, :, None], axis=1).T
    grad_logits = gates * (grad_gates - jnp.sum(gates * grad_gates, axis=1, keepdims=True))
    grad_logits_b = grad_logits.astype(jnp.bfloat16)
    grad_routed = jnp.einsum(
        "ecr,ecd->rd", dispatch_b, grad_back, preferred_element_type=jnp.float32
    )
    grad_routed = grad_routed + jnp.dot(
        grad_logits_b, w_router.T, preferred_element_type=jnp.float32
    )
    grad_w_router = jnp.dot(routed_in.T, grad_logits_b, preferred_element_type=jnp.float32)
    grad_norm_two, grad_gain_two = norm_backward(
        grad_routed, normed_two, scale_two, gain_two.astype(jnp.float32)
    )
    grad_mid = grad_out + grad_norm_two
    grad_mid_b = grad_mid.astype(jnp.bfloat16)
    grad_w_output = jnp.dot(mixed_b.T, grad_mid_b, preferred_element_type=jnp.float32)
    grad_mixed = jnp.dot(grad_mid_b, w_output.T, preferred_element_type=jnp.float32).reshape(
        rows, KV_HEADS, groups, HEAD_DIM
    )
    grad_mixed = (grad_mixed * live_rows[:, None, None, None]).astype(jnp.bfloat16)
    probs_again, unused_total = probabilities(query_b, key_b, allowed, log_total)
    grad_probs = jnp.einsum(
        "ikgd,jkd->kgij", grad_mixed, value_b, preferred_element_type=jnp.float32
    )
    delta = jnp.sum(probs_again * grad_probs, axis=-1, keepdims=True)
    grad_scores = (probs_again * (grad_probs - delta) * scale).astype(jnp.bfloat16)
    grad_query_raw = jnp.einsum(
        "kgij,jkd->ikgd", grad_scores, key_b, preferred_element_type=jnp.float32
    )
    grad_key_raw = jnp.einsum(
        "kgij,ikgd->jkd", grad_scores, query_b, preferred_element_type=jnp.float32
    )
    grad_value_raw = jnp.einsum(
        "kgij,ikgd->jkd",
        probs_again.astype(jnp.bfloat16),
        grad_mixed,
        preferred_element_type=jnp.float32,
    )
    grad_query_b = (
        unrotate(grad_query_raw, cos_query, sin_query)
        .reshape(rows, HEADS * HEAD_DIM)
        .astype(jnp.bfloat16)
    )
    grad_key_b = (
        unrotate(grad_key_raw, cos_key, sin_key)
        .reshape(rows, KV_HEADS * HEAD_DIM)
        .astype(jnp.bfloat16)
    )
    grad_value_b = grad_value_raw.reshape(rows, KV_HEADS * HEAD_DIM).astype(jnp.bfloat16)
    grad_w_query = jnp.dot(normed_in.T, grad_query_b, preferred_element_type=jnp.float32)
    grad_w_key = jnp.dot(normed_in.T, grad_key_b, preferred_element_type=jnp.float32)
    grad_w_value = jnp.dot(normed_in.T, grad_value_b, preferred_element_type=jnp.float32)
    grad_normed = jnp.dot(grad_query_b, w_query.T, preferred_element_type=jnp.float32)
    grad_normed = grad_normed + jnp.dot(grad_key_b, w_key.T, preferred_element_type=jnp.float32)
    grad_normed = grad_normed + jnp.dot(grad_value_b, w_value.T, preferred_element_type=jnp.float32)
    grad_norm_one, grad_gain_one = norm_backward(
        grad_normed, normed_one, scale_one, gain_one.astype(jnp.float32)
    )
    grad_input = (grad_mid + grad_norm_one).astype(jnp.bfloat16)
    grad_small = jnp.concatenate(
        [grad_w_router, grad_gain_one[:, None], grad_gain_two[:, None]], axis=1
    )
    grad_small = jnp.pad(grad_small, ((0, 0), (0, small_width - grad_small.shape[1])))
    blocks = sizes[0] * sizes[1]
    own_query, own_key, own_value, own_output, own_small = scatter_rows(
        sizes,
        [
            part.astype(jnp.bfloat16).reshape(blocks, -1, part.shape[1])
            for part in (grad_w_query, grad_w_key, grad_w_value, grad_w_output, grad_small)
        ],
    )
    dense_grads = (
        own_small[:, experts_all],
        own_query,
        own_key,
        own_value,
        own_output,
        own_small[:, experts_all + 1],
        own_small[:, :experts_all],
    )
    return (
        layer_out,
        grad_input,
        dense_grads[0],
        dense_grads[1],
        dense_grads[2],
        dense_grads[3],
        dense_grads[4],
        dense_grads[5],
        dense_grads[6],
        expert_grads[0],
        expert_grads[1],
        expert_grads[2],
    )


def solution(mesh):
    in_specs = (
        P(("dp", "fsdp"), None),
        P(("dp", "fsdp")),
        P(("dp", "fsdp"), None),
        P(("dp", "fsdp"), None),
        P(("dp", "fsdp")),
        P(("dp", "fsdp"), None),
        P(("dp", "fsdp"), None),
        P(("dp", "fsdp"), None),
        P(("dp", "fsdp"), None),
        P(("dp", "fsdp")),
        P(("dp", "fsdp"), None),
        P("dp", "fsdp", None),
        P("dp", "fsdp", None),
        P("dp", "fsdp", None),
    )
    out_specs = (
        P(("dp", "fsdp"), None),
        P(("dp", "fsdp"), None),
        P(("dp", "fsdp")),
        P(("dp", "fsdp"), None),
        P(("dp", "fsdp"), None),
        P(("dp", "fsdp"), None),
        P(("dp", "fsdp"), None),
        P(("dp", "fsdp")),
        P(("dp", "fsdp"), None),
        P("dp", "fsdp", None),
        P("dp", "fsdp", None),
        P("dp", "fsdp", None),
    )
    sizes = (mesh.shape["dp"], mesh.shape["fsdp"])
    body = functools.partial(shards, sizes)
    return jax.shard_map(body, mesh=mesh, in_specs=in_specs, out_specs=out_specs, check_vma=False)
```

time: 306 us -> 342 us (1.12)
  Pallas kernels: 105 us -> 230 us
  waiting for transfers between devices: 42.4 us -> 0 us
  blocking collectives: 25.3 us -> 0 us
  starting transfers between devices: 15.3 us -> 0 us
  local copies, waits for them, and re-layouts: 21.6 us -> 36.9 us
  between operations: 15 us -> 1.85 us
  other arithmetic: 26.4 us -> 21.9 us
  matrix products: 53.6 us -> 50.1 us
    pallas_call x2 -> x4, Pallas kernels: 105 us -> 230 us  [the longest x1 122 us: front_gather(): pl.pallas_call(lambda *refs: front_kernel(sizes, count, *refs), out_shape...]
    all_to_all x3 -> x0, waiting for transfers between devices: 40.2 us -> none  [the longest x1 17.9 us: shards(): lax.all_to_all(send_rows, 'dp', split_axis=0, concat_axis=0, tiled=True)]
    all_to_all x1 -> x0, blocking collectives: 25.3 us -> none  [shards(): lax.all_to_all(grad_send, 'dp', split_axis=0, concat_axis=0, tiled=True)]
    unnamed x110 -> x203, local copies, waits for them, and re-layouts: 3.41 us -> 27.3 us
    all_to_all x3 -> x0, starting transfers between devices: 14.9 us -> none  [the longest x1 5.44 us: shards(): lax.all_to_all(out_rows.reshape(recv_rows.shape), 'dp', split_axis=0, con...]
    dot_general x0 -> x4, local copies, waits for them, and re-layouts: none -> 7.24 us  [the longest x1 2.65 us: shards(): jnp.dot(normed_in, w_query, preferred_element_type=jnp.float32)]
    concatenate x2 -> x0, local copies, waits for them, and re-layouts: 7.05 us -> none  [the longest x1 3.64 us: shards(): jnp.concatenate([grad_w_query.astype(jnp.bfloat16), grad_w_key.astype(jnp...]
    add x0 -> x6, other arithmetic: none -> 6.97 us  [the longest x3 4.89 us: shards(): lax.dynamic_index_in_dim(mine, own, axis=0, keepdims=True)]
  transfers between devices with their start and end apart: 9 -> 0, of which waited for: 3 -> 0; matrix products, arithmetic and copies ran while one was open for 30% -> 0% of each run, Pallas kernels for 34% -> 0%
where the time goes in v1:
time: 342 us; the launch traced here: 341 us
  Pallas kernels  230 us (67%)
  matrix products  50.1 us (15%)
  local copies, waits for them, and re-layouts  36.9 us (11%)
  other arithmetic  21.9 us (6%)
    pallas_call x1, Pallas kernels, front_gather(): pl.pallas_call(lambda *refs: front_kernel(sizes, count, *refs), out_shape...  122 us
    pallas_call x2, Pallas kernels, swap_rows(): pl.pallas_call(lambda *refs: swap_kernel(sizes, count, parts, *refs), out...  64.3 us
    pallas_call x1, Pallas kernels, scatter_rows(): pl.pallas_call(lambda *refs: scatter_kernel(sizes, count, *refs), out_sha...  43.9 us
    unnamed x203, local copies, waits for them, and re-layouts  27.3 us

profile of v1, /device:TPU:0, one launch (start us, length us, event | category | flops | bytes accessed | tf_op | source)
XLA Modules:
  0.0 341.0 jit_solution(12490234536961732414)
XLA Ops:
  5.1 1.3 convolution_convert_fusion.6.refs_8_
  6.4 1.0 copy-done.20
  7.5 1.0 copy-done.21
  8.5 1.0 copy-done.22
  12.8 122.1 %front_gather.1 = (bf16[32,32,1024]{2,1,0:T(8,128)(2,1)S(1)}, bf16[32,32,512]{2,1,0:T(8,128)(2,1)S(1)}, bf16[32,32,512]{2,1,0:T(8,128)(2,1)S(1)}, bf16[32,32,102...) custom-call(bf16[32,1024]{1,0:T(8,128)(2,1)S(1)} %copy-done.28, ...), custom_call_target="tpu_custom_call" | custom-call | tf_op jit(solution)/shard_map/front_gather/pallas_call | solution.py:367
  134.9 1.3 copy-done
  136.2 1.0 copy-done.7
  137.2 1.0 copy-done.12
  138.2 1.0 copy-done.15
  141.0 1.4 copy.60
  142.3 1.2 slice_convert_fusion
  143.6 1.2 copy.85
  144.8 1.1 fusion.40
  145.9 2.5 fusion.17
  148.4 2.7 copy.62
  151.1 2.6 fusion.59
  154.7 1.3 copy.61
  156.0 1.9 fusion.62
  158.7 1.3 fusion.9
  160.2 2.1 fusion.14
  162.3 2.8 multiply_reduce_fusion.4
  166.3 1.8 copy.86
  173.0 1.2 convolution_convert_fusion.5
  174.2 23.9 %swap_out.1 = bf16[16,24,1152]{2,1,0:T(8,128)(2,1)S(1)} custom-call(bf16[16,24,1152]{2,1,0:T(8,128)(2,1)S(1)} %pad_maximum_fusion.refs_0_), custom_call_target="tpu_custom_call" | custom-call | tf_op jit(solution)/shard_map/swap_out/pallas_call | solution.py:443
  198.8 1.4 fusion.25
  200.2 1.5 convolution_convert_fusion.4
  202.0 1.3 multiply_convert_fusion
  204.2 2.6 multiply_convert_fusion.1
  208.0 1.5 add_convert_fusion
  210.2 1.2 convert_element_type.269.refs_2_
  212.2 1.3 copy-done.37
  213.7 1.9 copy.81
  215.6 3.5 %fusion.132 = (bf16[2,256,1024]{2,1,0:T(8,128)(2,1)S(1)}, f32[2,256,1024]{2,1,0:T(8,128)}) fusion(bf16[2,256,384]{2,1,0:T(8,128)(2,1)} %bitcast.221, bf16[384,1024,1]{1,0,2:T(8,128)(2,1)} %bitcast.218), kind=kOutput, calls=%fused_computation.214 | convolution fusion | flops 403177472 | bytes 4325376 | tf_op jit(solution)/shard_map/dot_general | solution.py:123
  219.2 40.4 %swap_back.1 = (bf16[16,24,1024]{2,1,0:T(8,128)(2,1)S(1)}, bf16[16,24,1024]{2,1,0:T(8,128)(2,1)S(1)}, bf16[1,512,512]{2,1,0:T(8,128)(2,1)S(1)}, bf16[1,512,512]{...) custom-call(bf16[16,24,1024]{2,1,0:T(8,128)(2,1)S(1)} %bitcast.202, bf16[16,24,1024]{2,1,0:T(8,128)(2,1)S(1)} %bitcast.196, ...), custom_call_target="tpu_custom_call" | custom-call | tf_op jit(solution)/shard_map/swap_back/pallas_call | solution.py:443
  260.0 1.1 fusion.13
  263.1 1.3 fusion.8
  266.9 3.2 convolution_bitcast_fusion.1
  270.0 1.1 multiply_add_fusion.1
  271.9 1.6 fusion.134
  273.6 2.6 convolution_bitcast_fusion.6
  276.8 2.2 fusion.16
  282.0 2.5 convolution_convert_fusion.2
  284.5 2.0 convolution_convert_fusion
  287.0 1.2 copy-done.4
  288.2 43.9 %scatter_rows.1 = (f32[32,1024]{1,0:T(8,128)S(1)}, f32[32,512]{1,0:T(8,128)S(1)}, f32[32,512]{1,0:T(8,128)S(1)}, f32[32,1024]{1,0:T(8,128)S(1)}, f32[32,128]{1,0:T(8,128)S(1)}) custom-call(bf16[32,32,1024]{2,1,0:T(8,128)(2,1)S(1)} %bitcast.177, bf16[32,32,512]{2,1,0:T(8,128)(2,1)S(1)} %bitcast.187, bf16[32,32,512]{2,1,0:T(8,128)(2,1)S(1)} %bitcast.188, ...), custom_call_target="tpu_custom_call" | custom-call | tf_op jit(solution)/shard_map/scatter_rows/pallas_call | solution.py:511
  333.5 2.7 convert_add_fusion.2
  336.2 1.1 convert_add_fusion.1
  337.3 1.1 convert_add_fusion
  (248 shorter events, 35.2 us)
Async XLA Ops:
  12.8 122.1 %copy-start.2 = (bf16[16,24,1024]{2,1,0:T(8,128)(2,1)}, bf16[16,24,1024]{2,1,0:T(8,128)(2,1)S(1)}, u32[]{:S(2)}) copy-start(bf16[16,24,1024]{2,1,0:T(8,128)(2,1)S(1)} %convolution_convert_fusion.6.refs_8_) | copy-start | bytes 2359300
  141.0 3.8 %copy-start.5 = (bf16[32,32,512]{2,1,0:T(8,128)(2,1)}, bf16[32,32,512]{2,1,0:T(8,128)(2,1)S(1)}, u32[]{:S(2)}) copy-start(bf16[32,32,512]{2,1,0:T(8,128)(2,1)S(1)} %get-tuple-element.32) | copy-start | bytes 3145732
  144.8 6.3 %copy-start.68 = (f32[1024,1]{0,1:T(1,128)}, f32[1024,1]{0,1:T(1,128)S(1)}, u32[]{:S(2)}) copy-start(f32[1024,1]{0,1:T(1,128)S(1)} %copy.85) | copy-start | bytes 12292
  145.9 5.2 %copy-start.81 = (f32[128]{0:T(128)}, f32[128]{0:T(128)S(1)}, u32[]{:S(2)}) copy-start(f32[128]{0:T(128)S(1)} %add_rsqrt_fusion.1) | copy-start | bytes 1540
  151.1 2.6 copy-start.90
  151.1 3.6 %copy-start.8 = (bf16[32,32,512]{2,1,0:T(8,128)(2,1)S(1)}, bf16[32,32,512]{2,1,0:T(8,128)(2,1)}, u32[]{:S(2)}) copy-start(bf16[32,32,512]{2,1,0:T(8,128)(2,1)} %copy-done.7) | copy-start | bytes 3145732
  156.0 2.7 copy-start.57
  156.0 4.1 %copy-start.91 = (s32[128]{0:T(128)S(1)}, s32[128]{0:T(128)}, u32[]{:S(2)}) copy-start(s32[128]{0:T(128)} %param.15) | copy-start | bytes 1540
  156.0 4.2 %copy-start.59 = (bf16[128,8,64,1]{0,2,3,1:T(8,128)(2,1)S(1)}, bf16[128,8,64,1]{0,2,3,1:T(8,128)(2,1)}, u32[]{:S(2)}) copy-start(bf16[128,8,64,1]{0,2,3,1:T(8,128)(2,1)} %fusion.17) | copy-start | bytes 393220
  156.0 4.2 %copy-start.93 = (f32[128]{0:T(128)S(1)}, f32[128]{0:T(128)}, u32[]{:S(2)}) copy-start(f32[128]{0:T(128)} %copy-done.92) | copy-start | bytes 1540
  157.9 4.4 %copy-start.34 = (bf16[128,1024]{1,0:T(8,128)(2,1)S(1)}, bf16[128,1024]{1,0:T(8,128)(2,1)}, u32[]{:S(2)}) copy-start(bf16[128,1024]{1,0:T(8,128)(2,1)} %param.14) | copy-start | bytes 786436
  158.7 3.6 %copy-start.70 = (bf16[128,8,32]{0,2,1:T(8,128)(2,1)}, bf16[128,8,32]{0,2,1:T(8,128)(2,1)S(1)}, u32[]{:S(2)}) copy-start(bf16[128,8,32]{0,2,1:T(8,128)(2,1)S(1)} %get-tuple-element.100) | copy-start | bytes 196612
  158.7 3.6 %copy-start.72 = (bf16[128,8,32]{0,2,1:T(8,128)(2,1)}, bf16[128,8,32]{0,2,1:T(8,128)(2,1)S(1)}, u32[]{:S(2)}) copy-start(bf16[128,8,32]{0,2,1:T(8,128)(2,1)S(1)} %get-tuple-element.101) | copy-start | bytes 196612
  162.3 7.9 %copy-start.55 = (bf16[8,64,2,128]{3,1,2,0:T(8,128)(2,1)}, bf16[8,64,2,128]{3,1,2,0:T(8,128)(2,1)S(1)}, u32[]{:S(2)}) copy-start(bf16[8,64,2,128]{3,1,2,0:T(8,128)(2,1)S(1)} %fusion.14) | copy-start | bytes 786436
  165.1 9.0 %copy-start.39 = (f32[128,1024]{1,0:T(8,128)}, f32[128,1024]{1,0:T(8,128)S(1)}, u32[]{:S(2)}) copy-start(f32[128,1024]{1,0:T(8,128)S(1)} %get-tuple-element.112) | copy-start | bytes 1572868
  170.2 4.0 %copy-start.45 = (bf16[128,1024]{1,0:T(8,128)(2,1)}, bf16[128,1024]{1,0:T(8,128)(2,1)S(1)}, u32[]{:S(2)}) copy-start(bf16[128,1024]{1,0:T(8,128)(2,1)S(1)} %multiply_convert_fusion.4) | copy-start | bytes 786436
  173.0 25.2 %copy-start.13 = (bf16[2,512,512]{2,1,0:T(8,128)(2,1)S(1)}, bf16[2,512,512]{2,1,0:T(8,128)(2,1)}, u32[]{:S(2)}) copy-start(bf16[2,512,512]{2,1,0:T(8,128)(2,1)} %copy-done.12) | copy-start | bytes 3145732
  174.2 24.5 %copy-start.16 = (bf16[2,512,512]{2,1,0:T(8,128)(2,1)S(1)}, bf16[2,512,512]{2,1,0:T(8,128)(2,1)}, u32[]{:S(2)}) copy-start(bf16[2,512,512]{2,1,0:T(8,128)(2,1)} %copy-done.15) | copy-start | bytes 3145732
  204.2 2.6 copy-start.14
  215.6 3.5 %copy-start.10 = (bf16[2,512,512]{2,1,0:T(8,128)(2,1)S(1)}, bf16[2,512,512]{2,1,0:T(8,128)(2,1)}, u32[]{:S(2)}) copy-start(bf16[2,512,512]{2,1,0:T(8,128)(2,1)} %convert_element_type.269.refs_2_) | copy-start | bytes 3145732
  215.6 3.5 %copy-start.11 = (bf16[384,1024]{1,0:T(8,128)(2,1)S(1)}, bf16[384,1024]{1,0:T(8,128)(2,1)}, u32[]{:S(2)}) copy-start(bf16[384,1024]{1,0:T(8,128)(2,1)} %add_convert_fusion) | copy-start | bytes 2359300
  215.6 3.5 %copy-start.18 = (bf16[384,1024]{1,0:T(8,128)(2,1)S(1)}, bf16[384,1024]{1,0:T(8,128)(2,1)}, u32[]{:S(2)}) copy-start(bf16[384,1024]{1,0:T(8,128)(2,1)} %convolution_convert_fusion.4) | copy-start | bytes 2359300
  219.1 40.5 %copy-start.65 = (f32[16,128]{1,0:T(8,128)S(1)}, f32[16,128]{1,0:T(8,128)}, u32[]{:S(2)}) copy-start(f32[16,128]{1,0:T(8,128)} %copy-done.64) | copy-start | bytes 24580
  219.1 40.5 %copy-start.67 = (f32[16,128]{1,0:T(8,128)S(1)}, f32[16,128]{1,0:T(8,128)}, u32[]{:S(2)}) copy-start(f32[16,128]{1,0:T(8,128)} %copy-done.66) | copy-start | bytes 24580
  219.1 40.5 %copy-start.74 = (f32[16,128]{1,0:T(8,128)S(1)}, f32[16,128]{1,0:T(8,128)}, u32[]{:S(2)}) copy-start(f32[16,128]{1,0:T(8,128)} %copy-done.73) | copy-start | bytes 24580
  219.2 40.8 %copy-start.40 = (f32[128,1024]{1,0:T(8,128)S(1)}, f32[128,1024]{1,0:T(8,128)}, u32[]{:S(2)}) copy-start(f32[128,1024]{1,0:T(8,128)} %copy-done.39) | copy-start | bytes 1572868
  263.1 2.7 copy-start.41
  263.1 3.4 copy-start.60
  266.5 3.5 %copy-start.63 = (f32[128,32]{0,1:T(8,128)S(1)}, f32[128,32]{0,1:T(8,128)}, u32[]{:S(2)}) copy-start(f32[128,32]{0,1:T(8,128)} %copy-done.62) | copy-start | bytes 49156
  266.8 4.4 %copy-start.52 = (f32[8,2,128,128]{2,3,1,0:T(8,128)}, f32[8,2,128,128]{2,3,1,0:T(8,128)S(1)}, u32[]{:S(2)}) copy-start(f32[8,2,128,128]{2,3,1,0:T(8,128)S(1)} %convolution_bitcast_fusion) | copy-start | bytes 3145732
  270.0 3.5 %copy-start.58 = (bf16[128,8,2,32]{0,3,2,1:T(8,128)(2,1)S(1)}, bf16[128,8,2,32]{0,3,2,1:T(8,128)(2,1)}, u32[]{:S(2)}) copy-start(bf16[128,8,2,32]{0,3,2,1:T(8,128)(2,1)} %get-tuple-element.97) | copy-start | bytes 393220
  271.9 4.3 %copy-start.9 = (bf16[32,32,512]{2,1,0:T(8,128)(2,1)S(1)}, bf16[32,32,512]{2,1,0:T(8,128)(2,1)}, u32[]{:S(2)}) copy-start(bf16[32,32,512]{2,1,0:T(8,128)(2,1)} %copy-done.7) | copy-start | bytes 3145732
  273.6 2.7 copy-start.50
  276.3 2.7 copy-start.6
  276.3 2.7 copy-start.35
  276.3 2.7 copy-start.69
  276.3 2.7 copy-start.82
  276.8 2.9 copy-start.42
  279.0 2.4 copy-start.61
  281.4 3.1 copy-start.43
  281.4 3.1 copy-start.56
  282.0 4.5 %copy-start.87 = (bf16[1024]{0:T(1024)(128)(2,1)S(1)}, bf16[1024]{0:T(1024)(128)(2,1)}, u32[]{:S(2)}) copy-start(bf16[1024]{0:T(1024)(128)(2,1)} %get-tuple-element.86) | copy-start | bytes 6148
  282.0 4.5 %copy-start.46 = (bf16[128,1024]{1,0:T(8,128)(2,1)S(1)}, bf16[128,1024]{1,0:T(8,128)(2,1)}, u32[]{:S(2)}) copy-start(bf16[128,1024]{1,0:T(8,128)(2,1)} %copy-done.45) | copy-start | bytes 786436
  282.0 4.5 %copy-start.79 = (bf16[128,16]{0,1:T(8,128)(2,1)S(1)}, bf16[128,16]{0,1:T(8,128)(2,1)}, u32[]{:S(2)}) copy-start(bf16[128,16]{0,1:T(8,128)(2,1)} %copy-done.78) | copy-start | bytes 12292
  332.2 4.1 %copy-start.26 = (bf16[1,512,512]{2,1,0:T(8,128)(2,1)S(1)}, bf16[1,512,512]{2,1,0:T(8,128)(2,1)}, u32[]{:S(2)}) copy-start(bf16[1,512,512]{2,1,0:T(8,128)(2,1)} %copy-done.25) | copy-start | bytes 1572868
  332.2 4.1 %copy-start.38 = (f32[1024,512]{1,0:T(8,128)S(1)}, f32[1024,512]{1,0:T(8,128)}, u32[]{:S(2)}) copy-start(f32[1024,512]{1,0:T(8,128)} %copy-done.37) | copy-start | bytes 6291460
  333.5 3.8 %copy-start.24 = (bf16[1,256,1024]{2,1,0:T(8,128)(2,1)S(1)}, bf16[1,256,1024]{2,1,0:T(8,128)(2,1)}, u32[]{:S(2)}) copy-start(bf16[1,256,1024]{2,1,0:T(8,128)(2,1)} %copy-done.23) | copy-start | bytes 1572868
  333.5 3.8 %copy-start.44 = (f32[2,256,1024]{2,1,0:T(8,128)S(1)}, f32[2,256,1024]{2,1,0:T(8,128)}, u32[]{:S(2)}) copy-start(f32[2,256,1024]{2,1,0:T(8,128)} %get-tuple-element.118) | copy-start | bytes 6291460
  (49 other events, 65.3 us)

commit v2 on v1

v2 whole, which is shorter than its diff:
```python
import functools

import jax
import jax.numpy as jnp
from jax import lax
from jax.experimental import pallas as pl
from jax.experimental.pallas import tpu as pltpu
from jax.sharding import PartitionSpec as P

HEADS = 16
KV_HEADS = 8
HEAD_DIM = 64
TOP = 8
CAP = 24


norm_eps = 1e-05


def slots_of(expert_block, live_rows, experts):
    row_count = expert_block.shape[0]
    chosen = jnp.sum(
        (expert_block[:, :, None] == jnp.arange(experts)[None, None, :]).astype(jnp.float32), axis=1
    )
    member = chosen * live_rows[:, None]
    lower = (jnp.arange(row_count)[None, :] < jnp.arange(row_count)[:, None]).astype(jnp.bfloat16)
    rank = jnp.dot(lower, member.astype(jnp.bfloat16), preferred_element_type=jnp.float32)
    kept = member * (rank < CAP).astype(jnp.float32)
    slot_match = (rank.T[:, None, :] == jnp.arange(CAP, dtype=jnp.float32)[None, :, None]).astype(
        jnp.float32
    )
    dispatch = kept.T[:, None, :] * slot_match
    return (dispatch, kept, chosen, rank)


def axis_bits(size):
    return size.bit_length() - 1


def span(bits):
    masks = [0]
    for bit in bits:
        masks = masks + [mask | (1 << bit) for mask in masks]
    return masks


def dimension_bits(sizes):
    dp_bits, fsdp_bits = (axis_bits(sizes[0]), axis_bits(sizes[1]))
    x_bits = list(range(fsdp_bits))
    high = [fsdp_bits + bit for bit in range(dp_bits - 1, 0, -1)]
    return {"x": x_bits, "z": high[:-1], "y": high[-1:], "c": [fsdp_bits] if dp_bits else []}


def bit_order(sizes, letters):
    bits = dimension_bits(sizes)
    return [bit for letter in letters for bit in bits[letter]]


class Cube:
    def __init__(self, sizes):
        self.sizes = sizes
        self.dp = lax.axis_index("dp")
        self.fsdp = lax.axis_index("fsdp")
        self.me = self.dp * sizes[1] + self.fsdp
        self.fsdp_bits = axis_bits(sizes[1])
        self.bits = axis_bits(sizes[0]) + self.fsdp_bits
        self.flips = [
            (1 - 2 * ((self.me // (1 << bit)) % 2)) * (1 << bit) for bit in range(self.bits)
        ]

    def block(self, mask):
        index = self.me
        for bit, flip in enumerate(self.flips):
            if mask >> bit & 1:
                index = index + flip
        return index

    def device(self, mask):
        other = self.block(mask)
        return {"dp": other // self.sizes[1], "fsdp": other % self.sizes[1]}

    def dp_masks(self):
        masks = [part << self.fsdp_bits for part in range(1, self.sizes[0])]
        return sorted(masks, reverse=True)

    def fsdp_masks(self):
        return list(range(1, self.sizes[1]))

    def greet(self, masks):
        barrier = pltpu.get_barrier_semaphore()
        for mask in masks:
            pl.semaphore_signal(
                barrier, inc=1, device_id=self.device(mask), device_id_type=pl.DeviceIdType.MESH
            )
        pl.semaphore_wait(barrier, len(masks))

    def send(self, source, target, send_sem, recv_sem, mask):
        copy = pltpu.make_async_remote_copy(
            src_ref=source,
            dst_ref=target,
            send_sem=send_sem,
            recv_sem=recv_sem,
            device_id=self.device(mask),
            device_id_type=pl.DeviceIdType.MESH,
        )
        copy.start()
        return copy


def link_of(sizes, bit):
    for letter, bits in dimension_bits(sizes).items():
        if bit in bits:
            return letter
    return "c"


def hop_time(sizes, bit, volume):
    bits = dimension_bits(sizes)
    if bit in bits["c"]:
        return volume / 6.0
    return volume * (1.5 if bit in bits["z"][:-1] else 1.0)


def gather_plan(sizes, orders, volumes, fills, lag, lead):
    free = {}
    known = [{0: 0.0} for _ in orders]
    waiting = []
    for which, order in enumerate(orders):
        for stage, bit in enumerate(order):
            for mask in span(order[:stage]):
                waiting.append((which, mask, bit, len(order) - stage))
    queues = {}
    for at, (link, volume) in enumerate(fills):
        queues.setdefault(link, []).append((at, volume))
    plan = []
    while waiting or any(queues.values()):
        best = None
        for item in waiting:
            which, mask, bit, left = item
            if mask in known[which]:
                begin = max(known[which][mask], free.get(link_of(sizes, bit), 0.0))
                rank = (begin, 0, -left, which, mask)
                if best is None or rank < best[0]:
                    best = (rank, item)
        for link, queue in queues.items():
            if queue:
                rank = (max(free.get(link, 0.0), 1e-6), 1, 0, 0, 0)
                if best is None or rank < best[0]:
                    best = (rank, (None, link))
        rank, item = best
        if item[0] is None:
            at, volume = queues[item[1]].pop(0)
            free[item[1]] = rank[0] + volume
            plan.append((rank[0] - lead, len(plan), (None, at, None)))
            continue
        which, mask, bit, _ = item
        end = rank[0] + hop_time(sizes, bit, volumes[which])
        free[link_of(sizes, bit)] = end
        known[which][mask | (1 << bit)] = end + lag
        plan.append((rank[0], len(plan), (which, mask, bit)))
        waiting.remove(item)
    return [step for _, _, step in sorted(plan)]


def scatter_plan(sizes, orders, volumes, lag):
    free = {}
    known = [{} for _ in orders]
    waiting = []
    for which, order in enumerate(orders):
        for stage, bit in enumerate(order):
            for rest in span(order[stage + 1 :]):
                waiting.append((which, stage, rest | (1 << bit)))
    plan = []
    while waiting:
        best = None
        for item in waiting:
            which, stage, mask = item
            needs = [mask | (1 << earlier) for earlier in orders[which][:stage]]
            if any(need not in known[which] for need in needs):
                continue
            bit = orders[which][stage]
            ready = max([known[which][need] for need in needs], default=0.0)
            begin = max(ready, free.get(link_of(sizes, bit), 0.0))
            after = [at for at, later in enumerate(orders[which]) if mask >> later & 1 and at > stage]
            rank = (begin, after[0] if after else len(orders[which]), which, mask)
            if best is None or rank < best[0]:
                best = (rank, item)
        rank, item = best
        which, stage, mask = item
        bit = orders[which][stage]
        end = rank[0] + hop_time(sizes, bit, volumes[which])
        free[link_of(sizes, bit)] = end
        known[which][mask] = end + lag
        plan.append(item)
        waiting.remove(item)
    return plan


def volume_of(shape):
    total = 1
    for size in shape:
        total = total * size
    return total


EXPERT_PIECES = 4
GATHER_LAG = 5.0
GATHER_LEAD = 1.0
GATHER_ORDERS = ("xzyc", "xzyc", "xzyc", "zxyc", "xzyc")
SCATTER_LAG = 1.5
SCATTER_ORDERS = ("zyxc", "xyzc", "zyxc", "zxyc", "zxyc")


def front_kernel(sizes, count, *refs):
    shards, experts, rows = (refs[:count], refs[count : count + 3], refs[count + 3])
    outs = refs[count + 4 :]
    full, wide, rows_out = (outs[:count], outs[count : count + 3], outs[count + 3])
    local_sems, send_sems, recv_sems, wide_send, wide_recv, row_send, row_recv = outs[count + 4 :]
    cube = Cube(sizes)
    singles = [1 << bit for bit in range(cube.bits)]
    cube.greet(sorted(set(singles + cube.dp_masks() + cube.fsdp_masks())))
    own = []
    for which, (source, target) in enumerate(zip(shards, full)):
        own.append((source, target.at[cube.me]))
    for which, (source, target) in enumerate(zip(experts, wide)):
        own.append((source, target.at[cube.fsdp]))
    own.append((rows.at[cube.dp], rows_out.at[cube.dp]))
    pending = []
    fills = []
    letters = dimension_bits(sizes)
    for piece in range(EXPERT_PIECES):
        for which, source in enumerate(experts):
            for mask in cube.fsdp_masks():
                volume = volume_of(source.shape) / EXPERT_PIECES
                fills.append(("x", volume, ("expert", which, mask, piece)))
    for peer in cube.dp_masks():
        link = [letter for letter in "zyc" if any(peer >> bit & 1 for bit in letters[letter])][0]
        fills.append((link, volume_of(rows.shape[1:]), ("row", peer)))

    def fill(kind, *rest):
        if kind == "expert":
            which, mask, piece = rest
            share = experts[which].shape[0] // EXPERT_PIECES
            place = pl.ds(piece * share, share)
            at = mask * EXPERT_PIECES + piece
            return cube.send(
                experts[which].at[place],
                wide[which].at[cube.fsdp, place],
                wide_send.at[which, at],
                wide_recv.at[which, at],
                mask,
            )
        peer = rest[0]
        part = peer >> cube.fsdp_bits
        return cube.send(
            rows.at[cube.block(peer) // sizes[1]],
            rows_out.at[cube.dp],
            row_send.at[part],
            row_recv.at[part],
            peer,
        )

    orders = [bit_order(sizes, letters) for letters in GATHER_ORDERS]
    unit = 46e3 / 2
    plan = gather_plan(
        sizes,
        orders,
        [volume_of(ref.shape) / unit for ref in shards],
        [(link, volume / unit) for link, volume, _ in fills],
        GATHER_LAG,
        GATHER_LEAD,
    )
    copies = [{} for _ in shards]
    arrived = [{0} for _ in shards]
    started = False
    for which, mask, bit in plan:
        if which is None:
            pending.append(fill(*fills[mask][2]))
            continue
        if mask and not started:
            started = True
            for at, (source, target) in enumerate(own):
                own[at] = pltpu.make_async_copy(source, target, local_sems.at[at])
                own[at].start()
        if mask not in arrived[which]:
            copies[which][mask].wait_recv()
            arrived[which].add(mask)
        label = mask | (1 << bit)
        target = full[which]
        copies[which][label] = cube.send(
            target.at[cube.block(mask)] if mask else shards[which],
            target.at[cube.block(mask)],
            send_sems.at[which, label],
            recv_sems.at[which, label],
            1 << bit,
        )
    for which, made in enumerate(copies):
        for label, copy in made.items():
            if label not in arrived[which]:
                copy.wait_recv()
    for copy in pending:
        copy.wait_recv()
    for copy in own:
        copy.wait()
    for made in copies:
        for copy in made.values():
            copy.wait_send()
    for copy in pending:
        copy.wait_send()


def front_gather(sizes, shards, experts, rows):
    blocks = sizes[0] * sizes[1]
    count = len(shards)
    out_shape = [jax.ShapeDtypeStruct((blocks,) + part.shape, part.dtype) for part in shards]
    out_shape += [jax.ShapeDtypeStruct((sizes[1],) + part.shape, part.dtype) for part in experts]
    out_shape += [jax.ShapeDtypeStruct(rows.shape, rows.dtype)]
    dma = pltpu.SemaphoreType.DMA
    return pl.pallas_call(
        lambda *refs: front_kernel(sizes, count, *refs),
        out_shape=tuple(out_shape),
        in_specs=[pl.BlockSpec(memory_space=pltpu.VMEM)] * (count + 4),
        out_specs=(pl.BlockSpec(memory_space=pl.ANY),) * (count + 4),
        scratch_shapes=[
            dma((count + 4,)),
            dma((count, blocks)),
            dma((count, blocks)),
            dma((3, sizes[1] * EXPERT_PIECES)),
            dma((3, sizes[1] * EXPERT_PIECES)),
            dma((sizes[0],)),
            dma((sizes[0],)),
        ],
        compiler_params=pltpu.CompilerParams(
            collective_id=0, has_side_effects=True, vmem_limit_bytes=24 * 1024 * 1024
        ),
        name="front_gather",
    )(*shards, *experts, rows)


def swap_kernel(sizes, count, parts, *refs):
    rows, grads = (refs[:count], refs[count : count + parts])
    outs = refs[count + parts :]
    rows_out, grads_out = (outs[:count], outs[count : count + parts])
    local_sems, row_send, row_recv, part_send, part_recv = outs[count + parts :]
    cube = Cube(sizes)
    cube.greet(cube.dp_masks() + (cube.fsdp_masks() if parts else []))
    pending = []
    for peer in cube.dp_masks():
        part = peer >> cube.fsdp_bits
        for which in range(count):
            pending.append(
                cube.send(
                    rows[which].at[cube.block(peer) // sizes[1]],
                    rows_out[which].at[cube.dp],
                    row_send.at[which, part],
                    row_recv.at[which, part],
                    peer,
                )
            )
    for mask in cube.fsdp_masks() if parts else []:
        for which in range(parts):
            pending.append(
                cube.send(
                    grads[which].at[cube.block(mask) % sizes[1]],
                    grads_out[which].at[mask - 1],
                    part_send.at[which, mask],
                    part_recv.at[which, mask],
                    mask,
                )
            )
    own = []
    for which in range(count):
        own.append(
            pltpu.make_async_copy(
                rows[which].at[cube.dp], rows_out[which].at[cube.dp], local_sems.at[which]
            )
        )
        own[-1].start()
    for copy in pending:
        copy.wait_recv()
    for copy in own:
        copy.wait()
    for copy in pending:
        copy.wait_send()


def swap_rows(sizes, rows, grads, collective_id, name):
    count, parts = (len(rows), len(grads))
    peers = max(sizes[1] - 1, 1)
    out_shape = [jax.ShapeDtypeStruct(part.shape, part.dtype) for part in rows]
    out_shape += [
        jax.ShapeDtypeStruct((peers,) + part.shape[1:], part.dtype) for part in grads
    ]
    dma = pltpu.SemaphoreType.DMA
    return pl.pallas_call(
        lambda *refs: swap_kernel(sizes, count, parts, *refs),
        out_shape=tuple(out_shape),
        in_specs=[pl.BlockSpec(memory_space=pltpu.VMEM)] * (count + parts),
        out_specs=(pl.BlockSpec(memory_space=pl.ANY),) * (count + parts),
        scratch_shapes=[
            dma((count,)),
            dma((count, sizes[0])),
            dma((count, sizes[0])),
            dma((max(parts, 1), sizes[1])),
            dma((max(parts, 1), sizes[1])),
        ],
        compiler_params=pltpu.CompilerParams(
            collective_id=collective_id,
            has_side_effects=True,
            vmem_limit_bytes=24 * 1024 * 1024,
        ),
        name=name,
    )(*rows, *grads)


def scatter_kernel(sizes, count, *refs):
    sources, outs = (refs[:count], refs[count : 2 * count])
    slots, held = (refs[2 * count : 3 * count], refs[3 * count : 4 * count])
    send_sems, recv_sems = refs[4 * count :]
    cube = Cube(sizes)
    cube.greet([1 << bit for bit in range(cube.bits)])
    orders = [bit_order(sizes, letters)[::-1] for letters in SCATTER_ORDERS]
    copies = [{} for _ in sources]
    arrived = [set() for _ in sources]
    places = [{} for _ in sources]

    def total(which, mask, stage):
        value = sources[which][cube.block(mask)].astype(jnp.float32)
        for earlier in orders[which][:stage]:
            label = mask | (1 << earlier)
            copies[which][label].wait_recv()
            value = value + slots[which][label].astype(jnp.float32)
        return value

    for which, stage, mask in scatter_plan(
        sizes, orders, [volume_of(ref.shape) / 23e3 for ref in outs], SCATTER_LAG
    ):
        if stage == 0:
            leaving = sources[which].at[cube.block(mask)]
        else:
            slot = places[which].setdefault(mask, len(places[which]))
            held[which][slot] = total(which, mask, stage).astype(jnp.bfloat16)
            leaving = held[which].at[slot]
        copies[which][mask] = cube.send(
            leaving,
            slots[which].at[mask],
            send_sems.at[which, mask],
            recv_sems.at[which, mask],
            1 << orders[which][stage],
        )
    for which in range(count):
        outs[which][...] = total(which, 0, len(orders[which]))
    for made in copies:
        for copy in made.values():
            copy.wait_send()


def scatter_rows(sizes, packed):
    blocks = sizes[0] * sizes[1]
    count = len(packed)
    shapes = [part.shape[1:] for part in packed]
    dma = pltpu.SemaphoreType.DMA
    return pl.pallas_call(
        lambda *refs: scatter_kernel(sizes, count, *refs),
        out_shape=tuple(jax.ShapeDtypeStruct(shape, jnp.float32) for shape in shapes),
        in_specs=[pl.BlockSpec(memory_space=pltpu.VMEM)] * count,
        out_specs=(pl.BlockSpec(memory_space=pltpu.VMEM),) * count,
        scratch_shapes=[pltpu.VMEM((blocks,) + shape, jnp.bfloat16) for shape in shapes]
        + [pltpu.VMEM((blocks // 2,) + shape, jnp.bfloat16) for shape in shapes]
        + [dma((count, blocks)), dma((count, blocks))],
        compiler_params=pltpu.CompilerParams(
            collective_id=3, has_side_effects=True, vmem_limit_bytes=48 * 1024 * 1024
        ),
        name="scatter_rows",
    )(*packed)


def lanes_of(shape):
    return lax.broadcasted_iota(jnp.int32, shape, 1)


def rows_of(shape):
    return lax.broadcasted_iota(jnp.int32, shape, 0)


def dot(left, right):
    return jnp.dot(left, right, preferred_element_type=jnp.float32)


def dot_nt(left, right):
    return lax.dot_general(
        left, right, (((1,), (1,)), ((), ())), preferred_element_type=jnp.float32
    )


def dot_tn(left, right):
    return lax.dot_general(
        left, right, (((0,), (0,)), ((), ())), preferred_element_type=jnp.float32
    )


def half(values):
    return values.astype(jnp.bfloat16)


def wide(values):
    return values.astype(jnp.float32)


def masks_of(doc_ref):
    count = doc_ref.shape[1]
    doc_row = jnp.broadcast_to(doc_ref[...].astype(jnp.float32), (count, count))
    doc_col = doc_row.T
    same = doc_row == doc_col
    row, lane = (rows_of((count, count)), lanes_of((count, count)))
    position = jnp.sum(jnp.where(same & (lane < row), 1.0, 0.0), axis=1, keepdims=True)
    allowed = same & (lane <= row)
    live = jnp.where(doc_col[:, :1] < count, 1.0, 0.0)
    return (position, allowed, live)


def slots_in_kernel(ids_ref, live, experts):
    count = ids_ref.shape[0]
    lane = lanes_of((count, 128))
    ids = ids_ref[...]
    chosen = jnp.zeros((count, 128), jnp.float32)
    for top in range(ids.shape[1]):
        chosen = chosen + jnp.where(ids[:, top : top + 1] == lane, 1.0, 0.0)
    member = chosen * live
    lower = jnp.where(lanes_of((count, count)) < rows_of((count, count)), 1.0, 0.0)
    rank = dot(half(lower), half(member))
    kept = jnp.where(rank < CAP, member, 0.0)
    place = jnp.where(kept > 0.0, rank, -1.0).T[:experts]
    slot = lax.broadcasted_iota(jnp.int32, (experts, CAP, count), 1).astype(jnp.float32)
    dispatch = jnp.where(place[:, None, :] == slot, 1.0, 0.0)
    return (chosen, dispatch)


def rope_in_kernel(position):
    lane = lanes_of((position.shape[0], 128))
    half_dim = HEAD_DIM // 2
    step = (lane % half_dim).astype(jnp.float32)
    freqs = jnp.exp(-jnp.log(10000.0) * (2.0 * step / HEAD_DIM))
    angle = position * freqs
    first = lane % HEAD_DIM < half_dim
    sinusoid = jnp.sin(angle)
    return (jnp.cos(angle), jnp.where(first, -sinusoid, sinusoid), first)


def swap_halves(values, first):
    width = values.shape[1]
    half_dim = HEAD_DIM // 2
    return jnp.where(
        first, pltpu.roll(values, width - half_dim, 1), pltpu.roll(values, half_dim, 1)
    )


def doubled(tile, odd):
    front = lanes_of(tile.shape) < HEAD_DIM
    rolled = pltpu.roll(tile, HEAD_DIM, 1)
    return half(jnp.where(front, rolled, tile) if odd else jnp.where(front, tile, rolled))


def stacked(tile):
    front = lanes_of(tile.shape) < HEAD_DIM
    return half(
        jnp.concatenate([jnp.where(front, tile, 0.0), jnp.where(front, 0.0, tile)], axis=0)
    )


def unstacked(pair):
    count = pair.shape[0] // 2
    front = lanes_of((count, pair.shape[1])) < HEAD_DIM
    return jnp.where(front, pair[:count], pair[count:])


def tile_of(at):
    return slice(128 * at, 128 * at + 128)


def small_rows(small_ref, experts):
    pick = jnp.where(lanes_of((8, 128)) == rows_of((8, 128)) + experts, 1.0, 0.0)
    picked = dot_nt(half(pick), small_ref[...])
    return (picked[0:1], picked[1:2])


def norm_in_kernel(values):
    scale_row = lax.rsqrt(jnp.mean(values * values, axis=1, keepdims=True) + norm_eps)
    return (values * scale_row, scale_row)


def forward_kernel(
    experts,
    hidden_ref,
    doc_ref,
    ids_ref,
    query_ref,
    key_ref,
    value_ref,
    output_ref,
    small_ref,
    rows_out,
    mid_out,
    q_out,
    k_out,
    v_out,
    p_out,
    o_out,
    routed_out,
    gates_out,
):
    scale = HEAD_DIM ** (-0.5)
    position, allowed, live = masks_of(doc_ref)
    chosen, dispatch = slots_in_kernel(ids_ref, live, experts)
    cosine, sinusoid, first = rope_in_kernel(position)
    gain_one, gain_two = small_rows(small_ref, experts)
    resid = wide(hidden_ref[...])
    normed, _ = norm_in_kernel(resid)
    h1 = half(normed * gain_one)
    key_raw = dot(h1, key_ref[...])
    for at in range(key_raw.shape[1] // 128):
        part = key_raw[:, tile_of(at)]
        k_out[:, tile_of(at)] = half(part * cosine + swap_halves(part, first) * sinusoid)
    v_out[...] = half(dot(h1, value_ref[...]))
    query_raw = dot(h1, query_ref[...])
    both = jnp.concatenate([allowed, allowed], axis=0)
    for head in range(KV_HEADS):
        part = query_raw[:, tile_of(head)]
        turned = half(part * cosine + swap_halves(part, first) * sinusoid)
        q_out[:, tile_of(head)] = turned
        keys = doubled(wide(k_out[:, tile_of(head // 2)]), head % 2)
        values = doubled(wide(v_out[:, tile_of(head // 2)]), head % 2)
        scores = dot_nt(stacked(wide(turned)), keys) * scale
        raised = jnp.where(both, jnp.exp(scores), 0.0)
        total = jnp.log(jnp.sum(raised, axis=1, keepdims=True))
        probs = jnp.where(both, jnp.exp(scores - total), 0.0)
        p_out[head] = probs
        o_out[:, tile_of(head)] = half(unstacked(dot(half(probs), values)) * live)
    mid = resid + dot(o_out[...], output_ref[...])
    mid_out[...] = mid
    normed_two, _ = norm_in_kernel(mid)
    h2 = half(normed_two * gain_two)
    routed_out[...] = h2
    logits = dot(h2, small_ref[...])
    raised = jnp.where(chosen > 0.0, jnp.exp(logits), 0.0)
    gates = raised / jnp.sum(raised, axis=1, keepdims=True)
    gates_t = gates.T[:experts]
    gates_out[...] = gates_t
    slots = experts * CAP
    one_hot = half(dispatch.reshape(slots, -1))
    slot_gate = jnp.sum(
        (dispatch * gates_t[:, None, :]).reshape(slots, -1), axis=1, keepdims=True
    )
    high = wide(half(slot_gate))
    middle = wide(half(slot_gate - high))
    low = slot_gate - high - middle
    lane = lanes_of((slots, 128))
    packed = jnp.where(
        lane == 0, high, jnp.where(lane == 1, middle, jnp.where(lane == 2, low, 0.0))
    )
    width = h2.shape[1]
    sent = dot(one_hot, h2)
    for e in range(experts):
        rows_out[e, :, :width] = half(sent[e * CAP : (e + 1) * CAP])
        rows_out[e, :, width:] = half(packed[e * CAP : (e + 1) * CAP])


def expert_kernel(rows_ref, grads_ref, gate_ref, up_ref, down_ref, out_ref, back_ref, *grads_out):
    width = grads_ref.shape[1]
    rows = rows_ref[:, :width]
    slot_gate = jnp.sum(wide(rows_ref[:, width:]), axis=1, keepdims=True)
    grad_rows = half(slot_gate * wide(grads_ref[...]))
    gate_pre = dot(rows, gate_ref[...])
    up_pre = dot(rows, up_ref[...])
    sigmoid_gate = 1.0 / (1.0 + jnp.exp(-gate_pre))
    act = half(gate_pre * sigmoid_gate * up_pre)
    out_ref[...] = half(dot(act, down_ref[...]))
    grad_act = dot_nt(grad_rows, down_ref[...])
    grad_up = half(grad_act * gate_pre * sigmoid_gate)
    grad_gate = half(grad_act * up_pre * sigmoid_gate * (1.0 + gate_pre * (1.0 - sigmoid_gate)))
    back_ref[...] = half(dot_nt(grad_gate, gate_ref[...]) + dot_nt(grad_up, up_ref[...]))
    made = (dot_tn(rows, grad_gate), dot_tn(rows, grad_up), dot_tn(act, grad_rows))
    for which, value in enumerate(made):
        grads_out[which][...] = value
        grads_out[which + 3][...] = half(value)


def backward_kernel(
    experts,
    hidden_ref,
    doc_ref,
    ids_ref,
    grad_ref,
    query_ref,
    key_ref,
    value_ref,
    output_ref,
    small_ref,
    mid_ref,
    q_ref,
    k_ref,
    v_ref,
    p_ref,
    o_ref,
    routed_ref,
    gates_ref,
    back_ref,
    slots_ref,
    layer_out,
    input_out,
    query_out,
    key_out,
    value_out,
    output_out,
    small_out,
    dq_ref,
    dk_ref,
    dv_ref,
):
    scale = HEAD_DIM ** (-0.5)
    position, _, live = masks_of(doc_ref)
    _, dispatch = slots_in_kernel(ids_ref, live, experts)
    cosine, sinusoid, first = rope_in_kernel(position)
    gain_one, gain_two = small_rows(small_ref, experts)
    slots = experts * CAP
    count = doc_ref.shape[1]
    gates = gates_ref[...]
    combine = (dispatch * gates[:, None, :]).reshape(slots, count).T
    combine_high = half(combine)
    combine_low = half(combine - wide(combine_high))
    flat = dispatch.reshape(slots, count)
    flat_t = half(flat.T)
    mid = mid_ref[...]
    out_rows = back_ref[...]
    layer_out[...] = half(mid + (dot(combine_high, out_rows) + dot(combine_low, out_rows)))
    row_dots = dot_nt(out_rows, grad_ref[...])
    grad_gates = jnp.sum((flat * row_dots).reshape(experts, CAP, count), axis=1)
    grad_logits = gates * (grad_gates - jnp.sum(gates * grad_gates, axis=0, keepdims=True))
    logit_rows = jnp.concatenate(
        [grad_logits, jnp.zeros((128 - experts, count), jnp.float32)], axis=0
    )
    logits_t = half(logit_rows.T)
    grad_router = dot(half(logit_rows), routed_ref[...])
    grad_routed = dot(flat_t, slots_ref[...]) + dot_nt(logits_t, small_ref[...])
    normed_two, scale_two = norm_in_kernel(mid)
    scaled = grad_routed * gain_two
    inner = jnp.mean(scaled * normed_two, axis=1, keepdims=True)
    grad_gain_two = jnp.sum(grad_routed * normed_two, axis=0, keepdims=True)
    grad_mid = wide(grad_ref[...]) + scale_two * (scaled - normed_two * inner)
    grad_mid_b = half(grad_mid)
    output_out[...] = half(dot_tn(o_ref[...], grad_mid_b))
    grad_mixed = half(dot_nt(grad_mid_b, output_ref[...]) * live)
    front = lanes_of((count, 128)) < HEAD_DIM
    pair = {}
    for head in range(KV_HEADS):
        keys = doubled(wide(k_ref[:, tile_of(head // 2)]), head % 2)
        values = doubled(wide(v_ref[:, tile_of(head // 2)]), head % 2)
        queries = stacked(wide(q_ref[:, tile_of(head)]))
        mixed = stacked(wide(grad_mixed[:, tile_of(head)]))
        probs = p_ref[head]
        grad_probs = dot_nt(mixed, values)
        delta = jnp.sum(probs * grad_probs, axis=1, keepdims=True)
        grad_scores = half(probs * (grad_probs - delta) * scale)
        part = unstacked(dot(grad_scores, keys))
        dq_ref[:, tile_of(head)] = half(part * cosine - swap_halves(part, first) * sinusoid)
        grad_key = dot_tn(grad_scores, queries)
        grad_value = dot_tn(half(probs), mixed)
        pair[head % 2] = (
            grad_key + pltpu.roll(grad_key, HEAD_DIM, 1),
            grad_value + pltpu.roll(grad_value, HEAD_DIM, 1),
        )
        if head % 2:
            part = jnp.where(front, pair[0][0], pair[1][0])
            dk_ref[:, tile_of(head // 2)] = half(
                part * cosine - swap_halves(part, first) * sinusoid
            )
            dv_ref[:, tile_of(head // 2)] = half(jnp.where(front, pair[0][1], pair[1][1]))
    resid = wide(hidden_ref[...])
    normed_one, scale_one = norm_in_kernel(resid)
    h1 = half(normed_one * gain_one)
    query_out[...] = half(dot_tn(h1, dq_ref[...]))
    key_out[...] = half(dot_tn(h1, dk_ref[...]))
    value_out[...] = half(dot_tn(h1, dv_ref[...]))
    grad_normed = dot_nt(dq_ref[...], query_ref[...])
    grad_normed = grad_normed + dot_nt(dk_ref[...], key_ref[...])
    grad_normed = grad_normed + dot_nt(dv_ref[...], value_ref[...])
    scaled = grad_normed * gain_one
    inner = jnp.mean(scaled * normed_one, axis=1, keepdims=True)
    grad_gain_one = jnp.sum(grad_normed * normed_one, axis=0, keepdims=True)
    input_out[...] = half(grad_mid + scale_one * (scaled - normed_one * inner))
    row = rows_of(grad_router.shape)
    small = jnp.where(
        row < experts,
        grad_router,
        jnp.where(row == experts, grad_gain_one, jnp.where(row == experts + 1, grad_gain_two, 0.0)),
    )
    small_out[...] = half(small.T)


def plain_call(kernel, name, outs, scratch, *args):
    return pl.pallas_call(
        kernel,
        out_shape=tuple(jax.ShapeDtypeStruct(shape, dtype) for shape, dtype in outs),
        in_specs=[pl.BlockSpec(memory_space=pltpu.VMEM)] * len(args),
        out_specs=(pl.BlockSpec(memory_space=pltpu.VMEM),) * len(outs),
        scratch_shapes=[pltpu.VMEM(shape, dtype) for shape, dtype in scratch],
        compiler_params=pltpu.CompilerParams(vmem_limit_bytes=60 * 1024 * 1024),
        name=name,
    )(*args)


def shards(
    sizes,
    hidden_in,
    doc_id,
    expert_ids,
    out_grad,
    attn_gain,
    query_weight,
    key_weight,
    value_weight,
    output_weight,
    ffn_gain,
    router_weight,
    expert_gate,
    expert_up,
    expert_down,
):
    rows, width = hidden_in.shape
    experts = router_weight.shape[1]
    blocks = sizes[0] * sizes[1]
    query_width, key_width = (query_weight.shape[1], key_weight.shape[1])
    hidden_units = expert_gate.shape[2]
    small = jnp.concatenate([router_weight, attn_gain[:, None], ffn_gain[:, None]], axis=1)
    small = jnp.pad(small, ((0, 0), (0, 128 - small.shape[1])))
    doc_row = doc_id.reshape(1, rows)
    slots = experts * CAP
    bf16, f32 = (jnp.bfloat16, jnp.float32)
    live_rows = (doc_id < rows).astype(f32)
    dispatch, _, _, _ = slots_of(expert_ids, live_rows, experts)
    pulled_b = jnp.einsum(
        "ecr,rd->ecd", dispatch.astype(bf16), out_grad, preferred_element_type=f32
    ).astype(bf16)
    gathered = front_gather(
        sizes,
        (query_weight, key_weight, value_weight, output_weight, small),
        (expert_gate[0], expert_up[0], expert_down[0]),
        pulled_b,
    )
    dense = [part.reshape(-1, part.shape[2]) for part in gathered[:5]]
    wide_experts = [part.reshape(-1, part.shape[2]) for part in gathered[5:8]]
    saved = plain_call(
        functools.partial(forward_kernel, experts),
        "forward",
        [
            ((experts, CAP, width + 128), bf16),
            ((rows, width), f32),
            ((rows, query_width), bf16),
            ((rows, key_width), bf16),
            ((rows, key_width), bf16),
            ((KV_HEADS, 2 * rows, rows), f32),
            ((rows, query_width), bf16),
            ((rows, width), bf16),
            ((experts, rows), f32),
        ],
        [],
        hidden_in,
        doc_row,
        expert_ids,
        *dense,
    )
    (recv,) = swap_rows(sizes, (saved[0],), (), 1, "swap_out")
    made = plain_call(
        expert_kernel,
        "experts",
        [((slots, width), bf16)] * 2
        + [((width, hidden_units), f32)] * 2
        + [((hidden_units, width), f32)]
        + [((width, hidden_units), bf16)] * 2
        + [((hidden_units, width), bf16)],
        [],
        recv.reshape(slots, -1),
        gathered[8].reshape(slots, width),
        *wide_experts,
    )
    swapped = swap_rows(
        sizes,
        [part.reshape(experts, CAP, width) for part in made[:2]],
        [part.reshape((sizes[1], -1) + part.shape[1:]) for part in made[5:]],
        2,
        "swap_back",
    )
    own = lax.axis_index("fsdp")
    expert_grads = [
        lax.dynamic_index_in_dim(
            mine.reshape((sizes[1], -1) + mine.shape[1:]), own, axis=0, keepdims=True
        )
        + jnp.sum(other.astype(f32), axis=0, keepdims=True)
        for mine, other in zip(made[2:5], swapped[2:])
    ]
    results = plain_call(
        functools.partial(backward_kernel, experts),
        "backward",
        [
            ((rows, width), bf16),
            ((rows, width), bf16),
            ((width, query_width), bf16),
            ((width, key_width), bf16),
            ((width, key_width), bf16),
            ((query_width, width), bf16),
            ((width, 128), bf16),
        ],
        [((rows, query_width), bf16), ((rows, key_width), bf16), ((rows, key_width), bf16)],
        hidden_in,
        doc_row,
        expert_ids,
        out_grad,
        *dense,
        *saved[1:],
        swapped[0].reshape(slots, width),
        swapped[1].reshape(slots, width),
    )
    own_query, own_key, own_value, own_output, own_small = scatter_rows(
        sizes, [part.reshape(blocks, -1, part.shape[1]) for part in results[2:]]
    )
    return (
        results[0],
        results[1],
        own_small[:, experts],
        own_query,
        own_key,
        own_value,
        own_output,
        own_small[:, experts + 1],
        own_small[:, :experts],
        expert_grads[0],
        expert_grads[1],
        expert_grads[2],
    )


def solution(mesh):
    in_specs = (
        P(("dp", "fsdp"), None),
        P(("dp", "fsdp")),
        P(("dp", "fsdp"), None),
        P(("dp", "fsdp"), None),
        P(("dp", "fsdp")),
        P(("dp", "fsdp"), None),
        P(("dp", "fsdp"), None),
        P(("dp", "fsdp"), None),
        P(("dp", "fsdp"), None),
        P(("dp", "fsdp")),
        P(("dp", "fsdp"), None),
        P("dp", "fsdp", None),
        P("dp", "fsdp", None),
        P("dp", "fsdp", None),
    )
    out_specs = (
        P(("dp", "fsdp"), None),
        P(("dp", "fsdp"), None),
        P(("dp", "fsdp")),
        P(("dp", "fsdp"), None),
        P(("dp", "fsdp"), None),
        P(("dp", "fsdp"), None),
        P(("dp", "fsdp"), None),
        P(("dp", "fsdp")),
        P(("dp", "fsdp"), None),
        P("dp", "fsdp", None),
        P("dp", "fsdp", None),
        P("dp", "fsdp", None),
    )
    sizes = (mesh.shape["dp"], mesh.shape["fsdp"])
    body = functools.partial(shards, sizes)
    return jax.shard_map(body, mesh=mesh, in_specs=in_specs, out_specs=out_specs, check_vma=False)
```

time: 342 us -> 238 us (0.70)
  matrix products: 50.1 us -> 1.46 us
  Pallas kernels: 230 us -> 191 us
  other arithmetic: 21.9 us -> 6.91 us
    pallas_call x1, Pallas kernels: 122 us -> 56 us  [front_gather(): pl.pallas_call(lambda *refs: front_kernel(sizes, count, *refs), out_shape...]
    dot_general x35 -> x1, matrix products: 50 us -> 1.33 us  [shards(): jnp.einsum('ecr,rd->ecd', dispatch.astype(bf16), out_grad, preferred_elem...]
    pallas_call x0 -> x3, Pallas kernels: none -> 31.8 us  [plain_call(): pl.pallas_call(kernel, out_shape=tuple((jax.ShapeDtypeStruct(shape, dtype...]
    unnamed x203 -> x69, local copies, waits for them, and re-layouts: 27.3 us -> 34.9 us
    dot_general x4 -> x0, local copies, waits for them, and re-layouts: 7.24 us -> none  [the longest x1 2.65 us: shards(): jnp.dot(normed_in, w_query, preferred_element_type=jnp.float32)]
    pallas_call x1, Pallas kernels: 43.9 us -> 37.5 us  [scatter_rows(): pl.pallas_call(lambda *refs: scatter_kernel(sizes, count, *refs), out_sha...]
    convert_element_type x11 -> x1, other arithmetic: 6.34 us -> 0.66 us  [shards(): live_rows = (doc_id < rows).astype(f32)]
    reduce_sum x8 -> x0, other arithmetic: 3.88 us -> none  [the longest x1 1.3 us: probabilities(): log_total = jnp.log(jnp.sum(raised, axis=-1, keepdims=True))]
where the time goes in v2:
time: 238 us; the launch traced here: 237 us
  Pallas kernels  191 us (80%)
  local copies, waits for them, and re-layouts  37.1 us (16%)
  other arithmetic  6.91 us (3%)
    pallas_call x2, Pallas kernels, swap_rows(): pl.pallas_call(lambda *refs: swap_kernel(sizes, count, parts, *refs), out...  65.8 us
    pallas_call x1, Pallas kernels, front_gather(): pl.pallas_call(lambda *refs: front_kernel(sizes, count, *refs), out_shape...  56 us
    pallas_call x1, Pallas kernels, scatter_rows(): pl.pallas_call(lambda *refs: scatter_kernel(sizes, count, *refs), out_sha...  37.5 us
    unnamed x69, local copies, waits for them, and re-layouts  34.9 us
    pallas_call x3, Pallas kernels, plain_call(): pl.pallas_call(kernel, out_shape=tuple((jax.ShapeDtypeStruct(shape, dtype...  31.8 us
    add x2, other arithmetic, shards(): lax.dynamic_index_in_dim(mine.reshape((sizes[1], -1) + mine.shape[1:]), o...  5.41 us

profile of v2, /device:TPU:0, one launch (start us, length us, event | category | flops | bytes accessed | tf_op | source)
XLA Modules:
  0.0 237.4 jit_solution(15474969572879532182)
XLA Ops:
  0.7 0.8 convert_reduce_fusion
  1.4 0.7 compare_convert_fusion
  2.2 1.3 convolution_convert_fusion.refs_8_
  3.6 0.8 copy.40
  4.3 0.8 copy.41
  5.1 0.8 copy.42
  5.9 1.0 copy-done.21
  7.0 1.0 copy-done.22
  8.0 1.0 copy-done.23
  9.0 0.8 copy-done.25
  9.9 0.8 copy-done.26
  10.7 0.8 copy-done.27
  11.5 0.8 copy-done.28
  12.2 56.0 %front_gather.1 = (bf16[32,32,1024]{2,1,0:T(8,128)(2,1)S(1)}, bf16[32,32,512]{2,1,0:T(8,128)(2,1)S(1)}, bf16[32,32,512]{2,1,0:T(8,128)(2,1)S(1)}, bf16[32,32,102...) custom-call(bf16[32,1024]{1,0:T(8,128)(2,1)S(1)} %copy-done.25, ...), custom_call_target="tpu_custom_call" | custom-call | tf_op jit(solution)/shard_map/front_gather/pallas_call | solution.py:319
  68.3 1.3 copy-done
  69.6 1.3 copy-done.1
  70.9 1.0 copy-done.2
  71.9 1.0 copy-done.3
  72.9 0.7 copy-done.8
  73.6 1.0 copy-done.9
  74.6 1.0 copy-done.10
  75.5 1.0 copy-done.11
  76.5 0.9 copy-done.18
  77.4 0.7 copy.44.ids_ref
  78.1 7.7 %forward.1 = (bf16[16,24,1152]{2,1,0:T(8,128)(2,1)}, f32[128,1024]{1,0:T(8,128)}, bf16[128,1024]{1,0:T(8,128)(2,1)}, bf16[128,512]{1,0:T(8,128)(2,1)}, bf16[128,...) custom-call(bf16[128,1024]{1,0:T(8,128)(2,1)} %hidden_ref.3, ...), custom_call_target="tpu_custom_call" | custom-call | tf_op jit(solution)/shard_map/forward/pallas_call | solution.py:801
  85.9 1.2 copy-done.15
  87.0 25.1 %swap_out.1 = bf16[16,24,1152]{2,1,0:T(8,128)(2,1)S(1)} custom-call(bf16[16,24,1152]{2,1,0:T(8,128)(2,1)S(1)} %copy-done.15), custom_call_target="tpu_custom_call" | custom-call | tf_op jit(solution)/shard_map/swap_out/pallas_call | solution.py:395
  112.1 0.9 copy-done.4
  113.0 9.3 %experts.1 = (bf16[384,1024]{1,0:T(8,128)(2,1)}, bf16[384,1024]{1,0:T(8,128)(2,1)}, f32[1024,512]{1,0:T(8,128)}, f32[1024,512]{1,0:T(8,128)}, f32[512,1024]{1,0:...) custom-call(bf16[384,1152]{1,0:T(8,128)(2,1)} %bitcast.45, ...), custom_call_target="tpu_custom_call" | custom-call | tf_op jit(solution)/shard_map/experts/pallas_call | solution.py:801
  122.3 1.2 copy-done.12
  123.6 1.2 copy-done.13
  124.8 1.2 copy-done.14
  126.0 1.1 copy-done.19
  127.2 1.1 copy-done.20
  128.3 40.7 %swap_back.1 = (bf16[16,24,1024]{2,1,0:T(8,128)(2,1)S(1)}, bf16[16,24,1024]{2,1,0:T(8,128)(2,1)S(1)}, bf16[1,512,512]{2,1,0:T(8,128)(2,1)S(1)}, bf16[1,512,512]{...) custom-call(bf16[16,24,1024]{2,1,0:T(8,128)(2,1)S(1)} %bitcast.60, bf16[16,24,1024]{2,1,0:T(8,128)(2,1)S(1)} %bitcast.61, ...), custom_call_target="tpu_custom_call" | custom-call | tf_op jit(solution)/shard_map/swap_back/pallas_call | solution.py:395
  169.0 0.9 copy-done.16
  169.9 0.9 copy-done.17
  170.8 2.5 %convert_add_fusion = f32[1,256,1024]{2,1,0:T(8,128)} fusion(bf16[1,256,1024]{2,1,0:T(8,128)(2,1)S(1)} %get-tuple-element.97, f32[2,256,1024]{2,1,0:T(8,128)} %bitcast.68, s32[]{:T(128)S(6)} %select_n.7), kind=kLoop, calls=%fused_computation.1 | loop fusion | flops 524288 | bytes 2621444 | tf_op jit(solution)/shard_map/add | solution.py:895
  173.3 2.9 %convert_add_fusion.1 = (f32[1,512,512]{2,1,0:T(8,128)}, f32[1,512,512]{2,1,0:T(8,128)}) fusion(bf16[1,512,512]{2,1,0:T(8,128)(2,1)S(1)} %get-tuple-element.95, f32[2,512,512]{2,1,0:T(8,128)} %bitcast.70, s32[]{:T(128)S(6)} %select_n.7, bf16[1,512,512]{2,1,0:T(8,128)(2,1)S(1)} %get-tuple-element.93, f32[2,512,512]{2,1,0:T(8,128)S(1)} %bitcast.69), kind=kLoop, calls=%fused_computation.2 | loop fusion | flops 1048576 | bytes 5242884 | tf_op jit(solution)/shard_map/add | solution.py:895
  176.2 14.7 %backward.1 = (bf16[128,1024]{1,0:T(8,128)(2,1)}, bf16[128,1024]{1,0:T(8,128)(2,1)}, bf16[1024,1024]{1,0:T(8,128)(2,1)}, bf16[1024,512]{1,0:T(8,128)(2,1)}, bf16...) custom-call(bf16[128,1024]{1,0:T(8,128)(2,1)} %hidden_ref.3, s32[1,128]{1,0:T(1,128)} %bitcast.72, ...), custom_call_target="tpu_custom_call" | custom-call | tf_op jit(solution)/shard_map/backward/pallas_call | solution.py:801
  190.9 1.6 copy-done.5
  192.5 1.2 copy-done.6
  193.7 1.2 copy-done.7
  195.0 0.9 copy-done.24
  195.9 37.5 %scatter_rows.1 = (f32[32,1024]{1,0:T(8,128)S(1)}, f32[32,512]{1,0:T(8,128)S(1)}, f32[32,512]{1,0:T(8,128)S(1)}, f32[32,1024]{1,0:T(8,128)S(1)}, f32[32,128]{1,0:T(8,128)S(1)}) custom-call(bf16[32,32,1024]{2,1,0:T(8,128)(2,1)S(1)} %bitcast.46, bf16[32,32,512]{2,1,0:T(8,128)(2,1)S(1)} %bitcast.47, bf16[32,32,512]{2,1,0:T(8,128)(2,1)S(1)} %bitcast.48, ...), custom_call_target="tpu_custom_call" | custom-call | tf_op jit(solution)/shard_map/scatter_rows/pallas_call | solution.py:463
  233.5 0.7 copy.45
  234.1 0.7 slice_reduce_fusion
  234.8 0.7 copy.50
  (38 shorter events, 2.2 us)
Async XLA Ops:
  0.6 76.8 %copy-start.30 = (s32[128,8]{0,1:T(8,128)S(1)}, s32[128,8]{0,1:T(8,128)}, u32[]{:S(2)}) copy-start(s32[128,8]{0,1:T(8,128)} %param.16) | copy-start | bytes 12292
  5.9 1.0 copy-start.21
  7.0 1.0 copy-start.22
  8.0 1.0 copy-start.23
  9.0 0.8 copy-start.25
  9.9 0.8 copy-start.26
  10.7 0.8 copy-start.27
  11.5 0.8 copy-start.28
  68.3 1.3 copy-start
  69.6 1.3 copy-start.1
  70.9 1.0 copy-start.2
  71.9 1.0 copy-start.3
  72.9 0.7 copy-start.8
  73.6 1.0 copy-start.9
  74.6 1.0 copy-start.10
  75.5 1.0 copy-start.11
  76.5 0.9 copy-start.18
  85.8 1.2 copy-start.15
  112.1 0.9 copy-start.4
  122.3 1.2 copy-start.12
  123.6 1.2 copy-start.13
  124.8 1.2 copy-start.14
  126.0 1.1 copy-start.19
  127.2 1.1 copy-start.20
  169.0 0.9 copy-start.16
  169.9 0.9 copy-start.17
  170.8 2.5 %copy-start.29 = (f32[1024,512]{1,0:T(8,128)S(1)}, f32[1024,512]{1,0:T(8,128)}, u32[]{:S(2)}) copy-start(f32[1024,512]{1,0:T(8,128)} %get-tuple-element.92) | copy-start | bytes 6291460
  190.9 1.6 copy-start.5
  192.5 1.2 copy-start.6
  193.7 1.2 copy-start.7
  195.0 0.9 copy-start.24

commit v3 on v2

--- a/solution.py
+++ b/solution.py
@@ -144,14 +144,14 @@
                     best = (rank, item)
         for link, queue in queues.items():
             if queue:
-                rank = (max(free.get(link, 0.0), 1e-6), 1, 0, 0, 0)
+                rank = (max(free.get(link, 0.0), 1e-6) + queue[0][1], 1, 0, 0, 0)
                 if best is None or rank < best[0]:
                     best = (rank, (None, link))
         rank, item = best
         if item[0] is None:
             at, volume = queues[item[1]].pop(0)
-            free[item[1]] = rank[0] + volume
-            plan.append((rank[0] - lead, len(plan), (None, at, None)))
+            free[item[1]] = rank[0]
+            plan.append((rank[0] - volume - lead, len(plan), (None, at, None)))
             continue
         which, mask, bit, _ = item
         end = rank[0] + hop_time(sizes, bit, volumes[which])
@@ -716,6 +716,7 @@
     dq_ref,
     dk_ref,
     dv_ref,
+    ready=lambda which: None,
 ):
     scale = HEAD_DIM ** (-0.5)
     position, _, live = masks_of(doc_ref)
@@ -749,6 +750,7 @@
     grad_mid = wide(grad_ref[...]) + scale_two * (scaled - normed_two * inner)
     grad_mid_b = half(grad_mid)
     output_out[...] = half(dot_tn(o_ref[...], grad_mid_b))
+    ready(3)
     grad_mixed = half(dot_nt(grad_mid_b, output_ref[...]) * live)
     front = lanes_of((count, 128)) < HEAD_DIM
     pair = {}
@@ -779,8 +781,11 @@
     normed_one, scale_one = norm_in_kernel(resid)
     h1 = half(normed_one * gain_one)
     query_out[...] = half(dot_tn(h1, dq_ref[...]))
+    ready(0)
     key_out[...] = half(dot_tn(h1, dk_ref[...]))
+    ready(1)
     value_out[...] = half(dot_tn(h1, dv_ref[...]))
+    ready(2)
     grad_normed = dot_nt(dq_ref[...], query_ref[...])
     grad_normed = grad_normed + dot_nt(dk_ref[...], key_ref[...])
     grad_normed = grad_normed + dot_nt(dv_ref[...], value_ref[...])
@@ -795,6 +800,7 @@
         jnp.where(row == experts, grad_gain_one, jnp.where(row == experts + 1, grad_gain_two, 0.0)),
     )
     small_out[...] = half(small.T)
+    ready(4)
 
 
 def plain_call(kernel, name, outs, scratch, *args):
@@ -807,6 +813,349 @@
         compiler_params=pltpu.CompilerParams(vmem_limit_bytes=60 * 1024 * 1024),
         name=name,
     )(*args)
+
+
+class Flat:
+    def __init__(self, ref):
+        self.ref = ref
+
+    def __getitem__(self, at):
+        return self.ref[...].reshape(-1, self.ref.shape[-1])
+
+    def __setitem__(self, at, value):
+        self.ref[...] = value.reshape(self.ref.shape)
+
+
+class Slots:
+    def __init__(self, ref):
+        self.ref = ref
+
+    def __getitem__(self, at):
+        return half(wide(self.ref[...]).reshape(-1, self.ref.shape[-1]))
+
+
+def step_kernel(sizes, experts, *refs):
+    hidden, doc, ids, grad = refs[:4]
+    shards, router, gains, weights = (list(refs[4:8]), refs[8], refs[9:11], refs[11:14])
+    layer_out, input_out = refs[14:16]
+    outs, own_out, other_out = (refs[16:21], refs[21:24], refs[24:27])
+    full, wide_refs = (refs[27:32], refs[32:35])
+    small_src, pulled, pulled_in, rows_src, rows_in = refs[35:40]
+    y_src, x_src, y_in, x_in = refs[40:44]
+    saved = refs[44:52]
+    sums, sums_half = (refs[52:55], refs[55:58])
+    grads, slots, held = (refs[58:63], refs[63:68], refs[68:73])
+    turned = refs[73:76]
+    (
+        local_sems,
+        send_sems,
+        recv_sems,
+        wide_send,
+        wide_recv,
+        row_send,
+        row_recv,
+        part_send,
+        part_recv,
+        back_send,
+        back_recv,
+    ) = refs[76:]
+    cube = Cube(sizes)
+    width = hidden.shape[1]
+    singles = [1 << bit for bit in range(cube.bits)]
+    cube.greet(sorted(set(singles + cube.dp_masks() + cube.fsdp_masks())))
+    local = []
+
+    def keep(source, target):
+        local.append(pltpu.make_async_copy(source, target, local_sems.at[len(local)]))
+        local[-1].start()
+        return local[-1]
+
+    depth = router.shape[0]
+    eye = lanes_of((depth, depth)) == rows_of((depth, depth))
+    lane = lanes_of((depth, 128))
+    pick = jnp.where(lanes_of((experts, 128)) == rows_of((experts, 128)), 1.0, 0.0)
+    small = dot(router[...], half(pick))
+    for at, gain in enumerate(gains):
+        column = jnp.sum(jnp.where(eye, wide(gain[...]), 0.0), axis=1, keepdims=True)
+        small = jnp.where(lane == experts + at, column, small)
+    small_src[...] = half(small)
+    shards.append(small_src)
+
+    leaving = []
+    fills = []
+    letters = dimension_bits(sizes)
+    peers = sorted(cube.dp_masks())
+    for piece in range(EXPERT_PIECES):
+        for which, source in enumerate(weights):
+            for mask in cube.fsdp_masks():
+                volume = volume_of(source.shape) / EXPERT_PIECES
+                fills.append(("x", volume, ("expert", which, mask, piece)))
+    for peer in peers:
+        link = [letter for letter in "zyc" if any(peer >> bit & 1 for bit in letters[letter])][0]
+        fills.append((link, volume_of(pulled.shape[1:]), ("row", peer)))
+
+    def rows_to(peer, source, target, which):
+        part = peer >> cube.fsdp_bits
+        copy = cube.send(
+            source.at[cube.block(peer) // sizes[1]],
+            target.at[cube.dp],
+            row_send.at[which, part],
+            row_recv.at[which, part],
+            peer,
+        )
+        leaving.append(copy)
+        return copy
+
+    def fill(kind, *rest):
+        if kind == "row":
+            return rows_to(rest[0], pulled, pulled_in, 0)
+        which, mask, piece = rest
+        share = weights[which].shape[1] // EXPERT_PIECES
+        place = pl.ds(piece * share, share)
+        at = mask * EXPERT_PIECES + piece
+        leaving.append(
+            cube.send(
+                weights[which].at[0, place],
+                wide_refs[which].at[cube.fsdp, place],
+                wide_send.at[which, at],
+                wide_recv.at[which, at],
+                mask,
+            )
+        )
+        return leaving[-1]
+
+    def prepare():
+        for which, source in enumerate(shards):
+            keep(source, full[which].at[cube.me])
+        for which, source in enumerate(weights):
+            keep(source.at[0], wide_refs[which].at[cube.fsdp])
+        _, _, live = masks_of(doc)
+        _, dispatch = slots_in_kernel(ids, live, experts)
+        moved = dot(half(dispatch.reshape(experts * CAP, -1)), grad[...])
+        for e in range(experts):
+            pulled[e] = half(moved[e * CAP : (e + 1) * CAP])
+
+    orders = [bit_order(sizes, order) for order in STEP_ORDERS]
+    unit = 46e3 / 2
+    plan = gather_plan(
+        sizes,
+        orders,
+        [volume_of(ref.shape[1:]) / unit for ref in full],
+        [(link, volume / unit) for link, volume, _ in fills],
+        GATHER_LAG,
+        GATHER_LEAD,
+    )
+    made = [{} for _ in shards]
+    arrived = [{0} for _ in shards]
+    filled = []
+    started = False
+    for which, mask, bit in plan:
+        if not started and (fills[mask][2][0] == "row" if which is None else mask):
+            started = True
+            prepare()
+        if which is None:
+            filled.append(fill(*fills[mask][2]))
+            continue
+        if mask not in arrived[which]:
+            made[which][mask].wait_recv()
+            arrived[which].add(mask)
+        label = mask | (1 << bit)
+        target = full[which].at[cube.block(mask)]
+        made[which][label] = cube.send(
+            target if mask else shards[which],
+            target,
+            send_sems.at[0, which, label],
+            recv_sems.at[0, which, label],
+            1 << bit,
+        )
+        leaving.append(made[which][label])
+    for which, part in enumerate(made):
+        for label, copy in part.items():
+            if label not in arrived[which]:
+                copy.wait_recv()
+    for copy in local:
+        copy.wait()
+    dense = [Flat(ref) for ref in full]
+    forward_kernel(experts, hidden, doc, ids, *dense, rows_src, *saved)
+    coming = [rows_to(peer, rows_src, rows_in, 1) for peer in peers]
+    mine = [keep(pulled.at[cube.dp], pulled_in.at[cube.dp])]
+    mine.append(keep(rows_src.at[cube.dp], rows_in.at[cube.dp]))
+    for copy in filled + coming:
+        copy.wait_recv()
+    for copy in mine:
+        copy.wait()
+
+    packed = wide(rows_in[...]).reshape(experts * CAP, -1)
+    rows = half(packed[:, :width])
+    slot_gate = jnp.sum(packed[:, width:], axis=1, keepdims=True)
+    grad_rows = half(slot_gate * wide(pulled_in[...]).reshape(experts * CAP, -1))
+    w_gate, w_up, w_down = [Flat(ref)[...] for ref in wide_refs]
+    gate_pre = dot(rows, w_gate)
+    up_pre = dot(rows, w_up)
+    sigmoid_gate = 1.0 / (1.0 + jnp.exp(-gate_pre))
+    act = half(gate_pre * sigmoid_gate * up_pre)
+    grad_act = dot_nt(grad_rows, w_down)
+    grad_up = half(grad_act * gate_pre * sigmoid_gate)
+    grad_gate = half(grad_act * up_pre * sigmoid_gate * (1.0 + gate_pre * (1.0 - sigmoid_gate)))
+
+    def give(values, source, target, which):
+        for e in range(experts):
+            source[e] = half(values[e * CAP : (e + 1) * CAP])
+        copies = [rows_to(peer, source, target, which) for peer in peers]
+        return (copies, keep(source.at[cube.dp], target.at[cube.dp]))
+
+    coming, kept = give(dot(act, w_down), y_src, y_in, 2)
+    more, kept_more = give(dot_nt(grad_gate, w_gate) + dot_nt(grad_up, w_up), x_src, x_in, 3)
+    exchanged = []
+    pairs = ((rows, grad_gate), (rows, grad_up), (act, grad_rows))
+    for which, (left, right) in enumerate(pairs):
+        value = dot_tn(left, right).reshape(sums[which].shape)
+        sums[which][...] = value
+        sums_half[which][...] = half(value)
+        for mask in cube.fsdp_masks():
+            exchanged.append(
+                cube.send(
+                    sums_half[which].at[cube.block(mask) % sizes[1]],
+                    other_out[which].at[mask - 1],
+                    part_send.at[which, mask],
+                    part_recv.at[which, mask],
+                    mask,
+                )
+            )
+    last = [keep(sums[which].at[cube.fsdp], own_out[which]) for which in range(3)]
+    for copy in coming + more:
+        copy.wait_recv()
+    kept.wait()
+    kept_more.wait()
+
+    back_orders = [bit_order(sizes, order)[::-1] for order in SCATTER_ORDERS]
+    back = [{} for _ in grads]
+    seen = [{} for _ in grads]
+
+    def total(which, mask, stage):
+        value = wide(grads[which][cube.block(mask)])
+        for earlier in back_orders[which][:stage]:
+            label = mask | (1 << earlier)
+            back[which][label].wait_recv()
+            value = value + wide(slots[which][label])
+        return value
+
+    def pass_on(which, stage, mask):
+        if stage == 0:
+            going = grads[which].at[cube.block(mask)]
+        else:
+            slot = seen[which].setdefault(mask, len(seen[which]))
+            held[which][slot] = half(total(which, mask, stage))
+            going = held[which].at[slot]
+        back[which][mask] = cube.send(
+            going,
+            slots[which].at[mask],
+            back_send.at[which, mask],
+            back_recv.at[which, mask],
+            1 << back_orders[which][stage],
+        )
+        leaving.append(back[which][mask])
+
+    steps = scatter_plan(
+        sizes, back_orders, [volume_of(ref.shape) / 23e3 for ref in outs], SCATTER_LAG
+    )
+
+    def ready(which):
+        for step in steps:
+            if step[0] == which and step[1] == 0:
+                pass_on(*step)
+
+    backward_kernel(
+        experts,
+        hidden,
+        doc,
+        ids,
+        grad,
+        *dense,
+        *saved,
+        Slots(y_in),
+        Slots(x_in),
+        layer_out,
+        input_out,
+        *[Flat(ref) for ref in grads],
+        *turned,
+        ready=ready,
+    )
+    for step in steps:
+        if step[1]:
+            pass_on(*step)
+    for which, out in enumerate(outs):
+        out[...] = total(which, 0, len(back_orders[which]))
+    for copy in exchanged:
+        copy.wait_recv()
+        copy.wait_send()
+    for copy in last:
+        copy.wait()
+    for copy in leaving:
+        copy.wait_send()
+
+
+STEP_ORDERS = ("zyxc", "xyzc", "zyxc", "zxyc", "zxyc")
+
+
+def step_call(sizes, experts, streams, tokens, router, gains, weights):
+    hidden, doc, ids, grad = tokens
+    rows, width = hidden.shape
+    blocks = sizes[0] * sizes[1]
+    bf16, f32 = (jnp.bfloat16, jnp.float32)
+    shapes = [part.shape for part in streams] + [(router.shape[0], 128)]
+    query_width, key_width = (streams[0].shape[1], streams[1].shape[1])
+    shares = [part.shape[1:] for part in weights]
+    spread = [(sizes[1],) + share for share in shares]
+    slot_rows = (experts, CAP, width)
+    tail = (experts, CAP, width + 128)
+    others = max(sizes[1] - 1, 1)
+    vmem, any_space = (pl.BlockSpec(memory_space=pltpu.VMEM), pl.BlockSpec(memory_space=pl.ANY))
+    scratch = [((blocks,) + shape, bf16) for shape in shapes]
+    scratch += [(shape, bf16) for shape in spread]
+    scratch += [(shapes[-1], bf16), (slot_rows, bf16), (slot_rows, bf16), (tail, bf16), (tail, bf16)]
+    scratch += [(slot_rows, bf16)] * 4
+    scratch += [
+        ((rows, width), f32),
+        ((rows, query_width), bf16),
+        ((rows, key_width), bf16),
+        ((rows, key_width), bf16),
+        ((KV_HEADS, 2 * rows, rows), f32),
+        ((rows, query_width), bf16),
+        ((rows, width), bf16),
+        ((experts, rows), f32),
+    ]
+    scratch += [(shape, f32) for shape in spread] + [(shape, bf16) for shape in spread]
+    scratch += [((blocks,) + shape, bf16) for shape in shapes] * 2
+    scratch += [((blocks // 2,) + shape, bf16) for shape in shapes]
+    scratch += [((rows, query_width), bf16), ((rows, key_width), bf16), ((rows, key_width), bf16)]
+    dma = pltpu.SemaphoreType.DMA
+    sems = [
+        dma((16,)),
+        dma((1, 5, blocks)),
+        dma((1, 5, blocks)),
+        dma((3, sizes[1] * EXPERT_PIECES)),
+        dma((3, sizes[1] * EXPERT_PIECES)),
+        dma((4, sizes[0])),
+        dma((4, sizes[0])),
+        dma((3, sizes[1])),
+        dma((3, sizes[1])),
+        dma((5, blocks)),
+        dma((5, blocks)),
+    ]
+    outs = [((rows, width), bf16)] * 2 + [(shape, f32) for shape in shapes]
+    outs += [(share, f32) for share in shares] + [((others,) + share, bf16) for share in shares]
+    return pl.pallas_call(
+        lambda *refs: step_kernel(sizes, experts, *refs),
+        out_shape=tuple(jax.ShapeDtypeStruct(shape, dtype) for shape, dtype in outs),
+        in_specs=[vmem] * 4 + [any_space] * 4 + [vmem] * 3 + [any_space] * 3,
+        out_specs=(vmem,) * 7 + (any_space,) * 6,
+        scratch_shapes=[pltpu.VMEM(shape, dtype) for shape, dtype in scratch] + sems,
+        compiler_params=pltpu.CompilerParams(
+            collective_id=4, has_side_effects=True, vmem_limit_bytes=60 * 1024 * 1024
+        ),
+        name="step",
+    )(hidden, doc, ids, grad, *streams, router, *gains, *weights)
 
 
 def shards(
@@ -830,6 +1179,30 @@
     experts = router_weight.shape[1]
     blocks = sizes[0] * sizes[1]
     query_width, key_width = (query_weight.shape[1], key_weight.shape[1])
+    if query_weight.shape[0] % 16 == 0:
+        step = step_call(
+            sizes,
+            experts,
+            (query_weight, key_weight, value_weight, output_weight),
+            (hidden_in, doc_id.reshape(1, rows), expert_ids, out_grad),
+            router_weight,
+            (attn_gain.reshape(1, -1), ffn_gain.reshape(1, -1)),
+            (expert_gate, expert_up, expert_down),
+        )
+        expert_grads = [
+            mine[None] + jnp.sum(other.astype(jnp.float32), axis=0, keepdims=True)
+            for mine, other in zip(step[7:10], step[10:13])
+        ]
+        own_small = step[6]
+        return (
+            step[0],
+            step[1],
+            own_small[:, experts],
+            *step[2:6],
+            own_small[:, experts + 1],
+            own_small[:, :experts],
+            *expert_grads,
+        )
     hidden_units = expert_gate.shape[2]
     small = jnp.concatenate([router_weight, attn_gain[:, None], ffn_gain[:, None]], axis=1)
     small = jnp.pad(small, ((0, 0), (0, 128 - small.shape[1])))

time: 238 us -> 171 us (0.72)
  Pallas kernels: 191 us -> 156 us
  local copies, waits for them, and re-layouts: 37.1 us -> 9.01 us
    pallas_call x7 -> x1, Pallas kernels: 191 us -> 156 us  [step_call(): pl.pallas_call(lambda *refs: step_kernel(sizes, experts, *refs), out_shap...]
    unnamed x69 -> x33, local copies, waits for them, and re-layouts: 34.9 us -> 8.31 us
where the time goes in v3:
time: 171 us
  Pallas kernels  156 us (91%)
  local copies, waits for them, and re-layouts  9.01 us (5%)
  other arithmetic  5.39 us (3%)
    pallas_call x1, Pallas kernels, step_call(): pl.pallas_call(lambda *refs: step_kernel(sizes, experts, *refs), out_shap...  156 us
    unnamed x33, local copies, waits for them, and re-layouts  8.31 us
    add x2, other arithmetic, shards(): mine[None] + jnp.sum(other.astype(jnp.float32), axis=0, keepdims=True)  5.39 us

profile of v3, /device:TPU:0, one launch (start us, length us, event | category | flops | bytes accessed | tf_op | source)
XLA Modules:
  0.0 171.1 jit_solution(6683346664538411880)
XLA Ops:
  0.6 0.0 copy-start.10
  0.7 0.7 copy-done.10
  1.3 0.0 copy-start.11
  1.3 0.7 copy.30.refs_8_
  2.0 0.0 copy-done.11
  2.0 0.7 copy.29.refs_2_
  2.7 156.0 %step.1 = (bf16[128,1024]{1,0:T(8,128)(2,1)}, bf16[128,1024]{1,0:T(8,128)(2,1)}, f32[32,1024]{1,0:T(8,128)}, f32[32,512]{1,0:T(8,128)}, f32[32,512]{1,0:T(8,128)...) custom-call(bf16[128,1024]{1,0:T(8,128)(2,1)} %refs_0_.1, ...), custom_call_target="tpu_custom_call" | custom-call | tf_op jit(solution)/shard_map/step/pallas_call | solution.py:1148
  158.7 0.0 copy-start.5
  158.7 0.7 copy-done.5
  159.5 0.7 slice_reduce_fusion
  160.1 0.7 copy.31
  160.8 0.0 copy-start
  160.8 0.0 copy-start.1
  160.8 0.0 copy-start.2
  160.8 2.7 %fusion = f32[1,256,1024]{2,1,0:T(8,128)} fusion(f32[256,1024]{1,0:T(8,128)} %get-tuple-element.36, bf16[1,256,1024]{2,1,0:T(8,128)(2,1)} %get-tuple-element.37), kind=kLoop, calls=%fused_computation.1 | loop fusion | flops 524288 | bytes 2621440 | tf_op jit(solution)/shard_map/add | solution.py:1193
  163.5 0.0 copy-done
  163.5 0.0 copy-done.1
  163.5 0.0 copy-done.2
  163.5 0.0 copy-start.4
  163.5 2.7 %fusion.1 = (f32[1,512,512]{2,1,0:T(8,128)}, f32[1,512,512]{2,1,0:T(8,128)}) fusion(f32[512,512]{1,0:T(8,128)S(1)} %copy-done.1, bf16[1,512,512]{2,1,0:T(8,128)(2,1)} %get-tuple-element.35, f32[512,512]{1,0:T(8,128)S(1)} %copy-done, bf16[1,512,512]{2,1,0:T(8,128)(2,1)S(1)} %copy-done.2), kind=kLoop, calls=%fused_computation.3 | loop fusion | flops 1048576 | bytes 5242880 | tf_op jit(solution)/shard_map/add | solution.py:1193
  166.2 0.0 copy-done.4
  166.2 0.0 copy-start.3
  166.2 0.7 copy.38
  166.9 0.3 copy-done.3
  167.3 0.0 copy-start.7
  167.3 0.7 copy.39
  168.0 0.3 copy-done.7
  168.3 0.0 copy-start.9
  168.3 0.0 copy-start.8
  168.3 0.7 copy.40
  168.9 0.2 copy-done.9
  169.1 0.0 copy-start.6
  169.1 0.6 copy.41
  169.8 0.0 copy-done.8
  169.8 0.6 copy.42
  170.4 0.0 copy-done.6
  170.4 0.7 copy.43
Async XLA Ops:
  0.6 0.7 copy-start.10
  1.3 0.7 copy-start.11
  158.7 0.7 copy-start.5
  160.8 2.7 %copy-start = (f32[512,512]{1,0:T(8,128)S(1)}, f32[512,512]{1,0:T(8,128)}, u32[]{:S(2)}) copy-start(f32[512,512]{1,0:T(8,128)} %get-tuple-element.32) | copy-start | bytes 3145732
  160.8 2.7 %copy-start.1 = (f32[512,512]{1,0:T(8,128)S(1)}, f32[512,512]{1,0:T(8,128)}, u32[]{:S(2)}) copy-start(f32[512,512]{1,0:T(8,128)} %get-tuple-element.34) | copy-start | bytes 3145732
  160.8 2.7 %copy-start.2 = (bf16[1,512,512]{2,1,0:T(8,128)(2,1)S(1)}, bf16[1,512,512]{2,1,0:T(8,128)(2,1)}, u32[]{:S(2)}) copy-start(bf16[1,512,512]{2,1,0:T(8,128)(2,1)} %get-tuple-element.33) | copy-start | bytes 1572868
  163.5 2.7 %copy-start.4 = (bf16[128,1024]{1,0:T(8,128)(2,1)S(1)}, bf16[128,1024]{1,0:T(8,128)(2,1)}, u32[]{:S(2)}) copy-start(bf16[128,1024]{1,0:T(8,128)(2,1)} %get-tuple-element.78) | copy-start | bytes 786436
  166.2 1.0 copy-start.3
  167.3 1.0 copy-start.7
  168.3 0.9 copy-start.9
  168.3 1.5 copy-start.8
  169.1 1.3 copy-start.6
